TPU v7x, 128 devices: a whole 4x4x4 slice. The times are simulated.
128 devices in a mesh: section: 8 (over x, core), seq: 16 (over z, y).
Axes of the slice: x: 4, y: 4, z: 4, core: 2. Of those that a mesh axis runs over, the one named last changes fastest.
Arguments:
- residual: bfloat16 [8, 4096, 2048], P('section', 'seq'), may hold values from -6 to 6
- w_qkv: bfloat16 [8, 2048, 6144], P('section', 'seq'), may hold values from -0.125 to 0.125
- w_beta: bfloat16 [8, 2048, 16], P('section', 'seq'), may hold values from -0.125 to 0.125
- beta_bias: float32 [8, 16], P('section'), may hold values from -8 to 2
- norm_gain: float32 [8, 2048], P('section'), may hold values from 0.1 to 1.9
- out_gain: float32 [8, 128], P('section'), may hold values from 0.1 to 1.9
- state_in: float32 [8, 16, 128, 128], P('section'), may hold values from -6 to 6
- doc_start: int32 [2, 8], P(None, 'section'), may hold values from 0 to 64, as said below
Outputs:
- stream_out: bfloat16 [8, 4096, 2048], P('section', 'seq')
Inputs may be any that keep to these rules, and one draw needn't show every extreme that they name: `doc_start`: 64 means no new document in that micro-batch.
All inputs are finite; a program needn't handle non-finite values.
Results may differ from a plain program's by a relative error of at most 0.03.
Values may be sent and summed in bfloat16 or wider, within the bound.
No kernel may reach another device: no remote copies, remote signals or barrier semaphores. Data moves between devices by JAX's collectives and lax.ppermute only.
A program may use at most 192 MiB of HBM per device.

v0:
```python
import functools

import jax
import jax.numpy as jnp
from jax import lax
from jax.experimental import pallas as pl
from jax.experimental.pallas import tpu as pltpu
from jax.sharding import Mesh, PartitionSpec as P

HEADS = 16
HD = 128
D = 2048
GROUP = 64
TICKS = 2
SIDE = 4
OWN = HEADS // SIDE
ROWS = 1024
CH = 128
BASE = 8
LEVELS = (8, 16, 32, 64)
PER = 4
GROUPS = ((0, 1), (2, 3))
BF = jnp.bfloat16
F32 = jnp.float32


def dot(a, b):
    return jnp.dot(a, b, preferred_element_type=F32)


def dot_nt(a, b):
    return lax.dot_general(a, b, (((1,), (1,)), ((), ())), preferred_element_type=F32)


def dot_tn(a, b):
    return lax.dot_general(a, b, (((0,), (0,)), ((), ())), preferred_element_type=F32)


def shift(value, axis, by, count=SIDE):
    return lax.ppermute(value, axis, [(i, (i + by) % count) for i in range(count)])


def around(value, axis, forward):
    left = shift(value, axis, 1)
    right = shift(value, axis, -1)
    across = shift(left, axis, 1) if forward else shift(right, axis, -1)
    return value, left, right, across


def after(value, *others):
    return lax.optimization_barrier((value, *others))[0]


STEPS = (0, -1, 1, 2)


def call(kernel, name, outs, ins, args, scratch=(), flops=0, vmem=16 << 20, grid=()):
    nbytes = sum(a.size * a.dtype.itemsize for a in args)
    return pl.pallas_call(
        kernel,
        out_shape=outs,
        in_specs=ins,
        out_specs=jax.tree.map(lambda _: pl.BlockSpec(memory_space=pltpu.VMEM), outs),
        scratch_shapes=list(scratch),
        grid=grid,
        name=name,
        compiler_params=pltpu.CompilerParams(vmem_limit_bytes=vmem),
        cost_estimate=pl.CostEstimate(flops=flops, bytes_accessed=nbytes, transcendentals=0),
    )(*args)


SM = pl.BlockSpec(memory_space=pltpu.SMEM)
VM = pl.BlockSpec(memory_space=pltpu.VMEM)
HBM = pl.BlockSpec(memory_space=pltpu.HBM)


def feature_block(where, p, s):
    z = lax.rem(where[0] + STEPS[p] + SIDE, SIDE)
    y = lax.rem(where[1] - s + SIDE, SIDE)
    return z * SIDE + y


def write_normed(where, read, scale, gain_ref, normed_ref, rows):
    for p in range(SIDE):
        for s in range(SIDE):
            at = pl.multiple_of(feature_block(where, p, s) * HD, HD)
            part = read(at).astype(F32) * scale * gain_ref[:, pl.ds(at, HD)]
            normed_ref[rows, (p * SIDE + s) * HD : (p * SIDE + s + 1) * HD] = part.astype(BF)


TILE = 128


def layer_kernel(tick, where, bias_ref, *refs):
    count = 1 if tick == 0 else SIDE * len(GROUPS)
    sources, refs = refs[:count], refs[count:]
    gain_ref, refs = refs[0], refs[1:]
    w_sources, refs = refs[: 5 * len(GROUPS)], refs[5 * len(GROUPS) :]
    p_ref, m_ref = refs[:2]
    res_ref, refs = (refs[2], refs[3:]) if tick == 0 else (None, refs[2:])
    x_ref, w0_ref, w1_ref, normed_ref, beta_ref, qkv_ref, state_ref, mask_ref, x_sems, w_sems = refs
    arrivals = []
    for at, ref in enumerate(sources):
        step = STEPS[at % SIDE]
        base = lax.rem(where[1] + step + SIDE, SIDE)
        if tick == 0:
            target = x_ref
        else:
            heads = GROUPS[at // SIDE]
            base = pl.multiple_of(base * (OWN * HD) + heads[0] * HD, HD)
            target = x_ref.at[:, pl.ds(base, len(heads) * HD)]
        arrivals.append(pltpu.make_async_copy(ref, target, x_sems.at[at]))
        arrivals[-1].start()
    w_arrivals = []
    for at, ref in enumerate(w_sources):
        start = (0, 512, 1024, 1536, 1792)[at % 5]
        target = (w0_ref, w1_ref)[at // 5].at[start : start + ref.shape[0]]
        w_arrivals.append(pltpu.make_async_copy(ref, target, w_sems.at[at]))
        w_arrivals[-1].start()

    for copy in arrivals:
        copy.wait()

    def normalize(i, carry):
        rows = pl.ds(pl.multiple_of(i * TILE, TILE), TILE)
        x = x_ref[rows, :].astype(F32)
        scale = lax.rsqrt(jnp.mean(x * x, axis=-1, keepdims=True) + 1e-05)
        write_normed(where, lambda at: x_ref[rows, pl.ds(at, HD)], scale, gain_ref, normed_ref, rows)
        if tick == 0:
            res_ref[rows, :] = x_ref[rows, pl.ds(pl.multiple_of(where[1] * 512, 512), 512)]
        return carry

    lax.fori_loop(0, ROWS // TILE, normalize, 0)
    for copy in w_arrivals:
        copy.wait()
    lane = lax.broadcasted_iota(jnp.int32, (1, HD), 1)
    bias = jnp.zeros((1, HD), F32)
    for h in range(OWN):
        bias = jnp.where(lane == h, bias_ref[0, where[1] * OWN + h], bias)
    logits = dot(normed_ref[...], w0_ref[:, 3 * len(GROUPS[0]) * HD :]) + bias
    beta_ref[...] = 1.0 / (1.0 + jnp.exp(-logits))

    width = len(GROUPS[0]) * HD
    for g in range(len(GROUPS)):
        def project(part, carry, g=g):
            cols = pl.ds(pl.multiple_of(part * width, width), width)
            acc = dot(normed_ref[...], (w0_ref, w1_ref)[g][:, cols])
            for h in range(width // HD):
                one = acc[:, h * HD : (h + 1) * HD]
                scale = lax.rsqrt(jnp.sum(one * one, axis=-1, keepdims=True) + 1e-06)
                scale = jnp.where(part < 2, scale, 1.0)
                qkv_ref[g, :, pl.ds(pl.multiple_of(part * width + h * HD, HD), HD)] = (one * scale).astype(BF)
            return carry

        lax.fori_loop(0, 3, project, 0)

    heads = range(OWN)
    nh = OWN
    row = lax.broadcasted_iota(jnp.int32, (CH, CH), 0)
    col = lax.broadcasted_iota(jnp.int32, (CH, CH), 1)
    lane = lax.broadcasted_iota(jnp.int32, (BASE, CH), 1)
    place = lax.broadcasted_iota(jnp.int32, (BASE, CH), 0)
    diagonal = (row // BASE) == (col // BASE)
    mask_ref[0] = jnp.where(diagonal, 1.0, 0.0)
    for level, size in enumerate(LEVELS):
        inside = (row // size) == (col // size) + 1
        mask_ref[level + 1] = jnp.where(inside, 1.0, 0.0)
    spread = jnp.where(diagonal, 1.0, 0.0).astype(BF)
    wide_col = lax.broadcasted_iota(jnp.int32, (CH, 2 * HD), 1)
    wide_row = lax.broadcasted_iota(jnp.int32, (CH, 2 * HD), 0)
    for h in range(nh):
        state_ref[h] = jnp.where(wide_col == wide_row, 1.0, 0.0)

    per = PER

    def chunks(i, carry):
        doc = where[2]
        items = [(c, h) for c in range(per) for h in range(nh)]
        base = [pl.multiple_of((i * per + c) * CH, CH) for c in range(per)]
        near = [doc - base[c] for c in range(per)]
        apart = [(col < near[c]) & (near[c] <= row) for c in range(per)]
        entry = [jnp.where((near[c] >= 0) & (near[c] <= row), 0.0, 1.0).astype(BF) for c in range(per)]
        leave = [jnp.where((row < near[c]) & (near[c] <= CH - 1), 0.0, 1.0).astype(BF) for c in range(per)]
        keep = [jnp.where((near[c] >= 0) & (near[c] <= CH - 1), 0.0, 1.0) for c in range(per)]
        rows = [pl.ds(base[c], CH) for c in range(per)]

        def part(c, h, which):
            at = (which * 2 + h % 2) * HD
            return qkv_ref[h // 2, rows[c], at : at + HD]

        q = [part(c, h, 0) for c, h in items]
        k = [part(c, h, 1) for c, h in items]
        v = [part(c, h, 2) for c, h in items]
        b = [jnp.broadcast_to(beta_ref[rows[c], heads[h] : heads[h] + 1], (CH, HD)) for c, h in items]
        n = range(len(items))
        both = [dot_nt(jnp.concatenate([q[t], k[t]], axis=0), k[t]) for t in n]
        attn, low = [], []
        for t, (c, h) in enumerate(items):
            attn.append(jnp.where((row >= col) & ~apart[c], both[t][:CH], 0.0).astype(BF))
            low.append(jnp.where((row > col) & ~apart[c], both[t][CH:] * b[t], 0.0))
        small = []
        for t in n:
            on = low[t] * mask_ref[0]
            small.append(sum(on[r * BASE : (r + 1) * BASE] for r in range(CH // BASE)))
        picked = [jnp.concatenate([jnp.where((lane & (BASE - 1)) == j, small[t], 0.0) for j in range(BASE)], axis=0) for t in n]
        factors = [dot(picked[t].astype(BF), spread) for t in n]
        tops = [jnp.where((lane & (BASE - 1)) == place, 1.0, 0.0) for t in n]
        for j in range(BASE - 1):
            tops = [tops[t] - factors[t][j * BASE : (j + 1) * BASE] * tops[t][j : j + 1] for t in n]
        inv = [jnp.concatenate([tops[t]] * (CH // BASE), axis=0) * mask_ref[0] for t in n]
        for level, size in enumerate(LEVELS):
            blocks = range(CH // size)

            def odd(value):
                return jnp.concatenate([value[r * size : (r + 1) * size] for r in blocks if r % 2], axis=0)

            def mixed(even, odds):
                pieces = []
                for r in blocks:
                    at = r // 2 * size
                    pieces.append(odds[at : at + size] if r % 2 else even(r))
                return jnp.concatenate(pieces, axis=0)

            below = [(odd(low[t]) * odd(mask_ref[level + 1])).astype(BF) for t in n]
            mid = [dot(below[t], inv[t].astype(BF)) for t in n]
            mid = [mixed(lambda r: jnp.zeros((size, CH), F32), mid[t]).astype(BF) for t in n]
            rest = [odd(inv[t]) for t in n]
            rest = [rest[t] - dot(rest[t].astype(BF), mid[t]) for t in n]
            inv = [mixed(lambda r: inv[t][r * size : (r + 1) * size], rest[t]) for t in n]
        right = []
        for t, (c, h) in enumerate(items):
            bk = (k[t].astype(F32) * b[t]).astype(BF) * entry[c]
            right.append(jnp.concatenate([bk, (v[t].astype(F32) * b[t]).astype(BF)], axis=1))
        wu = [dot(inv[t].astype(BF), right[t]) for t in n]
        weight = [wu[t][:, :HD].astype(BF) for t in n]
        inject = [jnp.concatenate([jnp.zeros((CH, HD), F32), wu[t][:, HD:]], axis=1) for t in n]
        left = [jnp.concatenate([q[t] * entry[c], attn[t]], axis=1) for t, (c, h) in enumerate(items)]
        kept = [k[t] * leave[c] for t, (c, h) in enumerate(items)]
        for t, (c, h) in enumerate(items):
            state = state_ref[h]
            short = state.astype(BF)
            delta = (inject[t] - dot(weight[t], short)).astype(BF)
            state_ref[h] = state * keep[c] + dot_tn(kept[t], delta)
            result = dot(left[t], jnp.concatenate([short, delta], axis=0))
            p_ref[rows[c], h * 2 * HD : (h + 1) * 2 * HD] = result.astype(BF)
        return carry

    lax.fori_loop(0, ROWS // CH // per, chunks, 0)
    for h in range(nh):
        m_ref[h] = state_ref[h].astype(BF)


def finish_kernel(nh, split, where, m0, m1, m2, m3, s_ref, p_ref, x_refs, gain_ref, out_refs, final_ref, maps_ref):
    for s, ref in enumerate((m0, m1, m2, m3)):
        maps_ref[lax.rem(where[0] - s + SIDE, SIDE)] = ref[...]
    states = [s_ref[h] for h in range(nh)]
    firsts = list(states)
    for z in range(SIDE):
        for h in range(nh):
            firsts[h] = jnp.where(where[0] == z, states[h], firsts[h])
        if split and z == SIDE - 1:
            break
        for h in range(nh):
            high = states[h].astype(BF)
            low = (states[h] - high.astype(F32)).astype(BF)
            a = maps_ref[z, h, :, :HD]
            states[h] = dot(a, high) + dot(a, low) + maps_ref[z, h, :, HD:].astype(F32)
    if not split:
        for h in range(nh):
            final_ref[h] = states[h]
    entries = [first.astype(BF) for first in firsts]

    def finish(rows, outs, out_rows):
        for h in range(nh):
            pa = p_ref[rows, h * 2 * HD : h * 2 * HD + HD]
            pb = p_ref[rows, h * 2 * HD + HD : (h + 1) * 2 * HD]
            o = dot(pa, entries[h]) + pb.astype(F32)
            o = o * lax.rsqrt(jnp.mean(o * o, axis=-1, keepdims=True) + 1e-05) * gain_ref[...]
            x_ref = x_refs[h * len(x_refs) // nh]
            at = h % (nh // len(x_refs)) * HD
            x = x_ref[rows, at : at + HD].astype(F32)
            at = h % (nh // len(outs)) * HD
            outs[h * len(outs) // nh][out_rows, at : at + HD] = (x + o).astype(BF)

    if split:
        for s in range(SIDE):
            rows = pl.ds(pl.multiple_of(lax.rem(where[1] + s, SIDE) * 256, 256), 256)
            finish(rows, out_refs[s : s + 1], slice(None))
    else:

        def block(i, carry):
            rows = pl.ds(pl.multiple_of(i * 256, 256), 256)
            finish(rows, out_refs, rows)
            return carry

        lax.fori_loop(0, ROWS // 256, block, 0)


def finish_first_kernel(nh, *refs):
    finish_kernel(nh, False, *refs[:7], (refs[7],), *refs[8:9], refs[9:11], *refs[11:])


def finish_last_kernel(nh, *refs):
    finish_kernel(nh, True, *refs[:7], refs[7:9], refs[9], refs[10:14], None, refs[14])


def pack_kernel(where, w_ref, wb_ref, *out_refs):
    for g, heads in enumerate(GROUPS):
        width = len(heads) * HD
        for s in range(SIDE):
            for part in range(3):
                at = part * D + lax.rem(where[1] + s, SIDE) * (OWN * HD) + heads[0] * HD
                columns = w_ref[:, pl.ds(pl.multiple_of(at, HD), width)]
                out_refs[g * SIDE + s][:, part * width : (part + 1) * width] = columns
    source = lax.broadcasted_iota(jnp.int32, (HEADS, HD), 0)
    target = lax.broadcasted_iota(jnp.int32, (HEADS, HD), 1)
    for s in range(SIDE):
        chosen = (source == target + lax.rem(where[1] + s, SIDE) * OWN) & (target < OWN)
        out_refs[s][:, 3 * len(GROUPS[0]) * HD :] = dot(wb_ref[...], jnp.where(chosen, 1.0, 0.0).astype(BF)).astype(BF)


def join_kernel(*refs):
    for s in range(SIDE):
        refs[-1][s * HD : (s + 1) * HD] = refs[s][...]


def place_kernel(where, *refs):
    for s in range(SIDE):
        at = lax.rem(where[1] - s + SIDE, SIDE) * (OWN * HD)
        refs[-1][:, pl.ds(pl.multiple_of(at, OWN * HD), OWN * HD)] = refs[s][...]


def struct(shape, dtype=BF):
    return jax.ShapeDtypeStruct(shape, dtype)


def shards(residual, w_qkv, w_beta, beta_bias, norm_gain, out_gain, state_in, doc_start):
    z, y = lax.axis_index("z"), lax.axis_index("y")
    here = jnp.stack([z, y]).astype(jnp.int32)

    width = 3 * len(GROUPS[0]) * HD
    widths = (width + HD, width)
    packs = [struct((HD, wide)) for wide in widths for _ in range(SIDE)]
    packed = call(pack_kernel, "pack", packs, [SM, VM, VM], (here, w_qkv[0], w_beta[0]))
    sent = []
    for g in range(len(GROUPS)):
        mine = packed[g * SIDE : g * SIDE + SIDE]
        if sent:
            mine = after(tuple(mine), *sent[-1][1:])
        sent.append([mine[0]] + [shift(mine[s], "y", s) for s in range(1, SIDE)])
    weights = []
    for g in range(len(GROUPS)):
        joined = call(join_kernel, "join", [struct((SIDE * HD, widths[g]))], [VM] * SIDE, tuple(sent[g]))[0]
        left, right = shift(joined, "z", 1), shift(joined, "z", -1)
        half = joined.shape[0] // 2
        weights.append((joined, left, right, shift(left[:half], "z", 1), shift(right[half:], "z", -1)))
    flat = [piece for pieces in weights for piece in pieces]
    x = after(residual[0], *sent[0][1:])
    pieces = [lax.all_gather(x, "y", axis=0, tiled=True)]
    states = lax.dynamic_slice_in_dim(state_in[0], y * OWN, OWN, axis=0)

    for tick in range(TICKS):
        where = jnp.stack([z, y, doc_start[tick, 0] * GROUP - z * ROWS]).astype(jnp.int32)
        outs = [struct((ROWS, OWN * 2 * HD)), struct((OWN, HD, 2 * HD))]
        scratch = [
            pltpu.VMEM((ROWS, D), BF),
            pltpu.VMEM((D, widths[0]), BF),
            pltpu.VMEM((D, widths[1]), BF),
            pltpu.VMEM((ROWS, D), BF),
            pltpu.VMEM((ROWS, HD), F32),
            pltpu.VMEM((len(GROUPS), ROWS, width), BF),
            pltpu.VMEM((OWN, HD, 2 * HD), F32),
            pltpu.VMEM((1 + len(LEVELS), CH, CH), F32),
            pltpu.SemaphoreType.DMA((len(pieces),)),
            pltpu.SemaphoreType.DMA((len(flat),)),
        ]
        if tick == 0:
            outs.append(struct((ROWS, OWN * HD)))
        p, m, *rest = call(
            functools.partial(layer_kernel, tick),
            "layer",
            outs,
            [SM, SM] + [HBM] * len(pieces) + [VM] + [HBM] * len(flat),
            (where, beta_bias, *pieces, norm_gain, *flat),
            scratch=scratch,
            flops=8 * ROWS * D * OWN * HD,
            vmem=60 << 20,
        )
        maps = [m] + [shift(m, "z", s) for s in range(1, SIDE)]
        if tick + 1 < TICKS:
            pieces = []
            *outs, states = call(
                functools.partial(finish_first_kernel, OWN),
                "finish",
                [struct((ROWS, OWN * HD // len(GROUPS)))] * len(GROUPS) + [struct((OWN, HD, HD), F32)],
                [SM] + [VM] * 8,
                (where, *maps, states, p, rest[0], out_gain),
                scratch=[pltpu.VMEM((SIDE, OWN, HD, 2 * HD), BF)],
            )
            moved = [shift(out, "section", 1, lax.axis_size("section")) for out in outs]
            for g in range(len(GROUPS)):
                pieces.extend(around(moved[g], "y", g == 0))
        else:
            outs = call(
                functools.partial(finish_last_kernel, OWN),
                "finish_last",
                [struct((256, OWN * HD))] * SIDE,
                [SM] + [VM] * 9,
                (where, *maps, states, p, pieces[0], pieces[SIDE], out_gain),
                scratch=[pltpu.VMEM((SIDE, OWN, HD, 2 * HD), BF)],
            )
    outs = [outs[0]] + [shift(outs[s], "y", s) for s in range(1, SIDE)]
    out = call(place_kernel, "place", [struct((256, D))], [SM] + [VM] * SIDE, (here, *outs))[0]
    return out[None]


def solution(mesh):
    split = Mesh(mesh.devices.reshape(mesh.devices.shape[0], SIDE, SIDE), ("section", "z", "y"))
    wide = P("section", ("z", "y"), None)
    return jax.shard_map(
        shards,
        mesh=split,
        in_specs=(
            wide,
            wide,
            wide,
            P("section", None),
            P("section", None),
            P("section", None),
            P("section", None, None, None),
            P(None, "section"),
        ),
        out_specs=wide,
        check_vma=False,
    )
```

profile of v0, /device:TPU:34, one launch (start us, length us, event | category | flops | bytes accessed | tf_op | source)
XLA Modules:
  0.0 263.9 jit_solution(2586772664171651396)
XLA Ops:
  6.5 0.9 copy.9
  7.5 1.4 copy-done.3
  8.9 1.5 pack.1
  10.4 1.6 collective-permute-start
  12.0 2.9 %collective-permute-start.1 = (bf16[128,896]{1,0:T(8,128)(2,1)S(1)}, bf16[128,896]{1,0:T(8,128)(2,1)S(1)}, u32[]{:S(2)}, u32[]{:S(2)}) collective-permute-start(bf16[128,896]{1,0:T(8,128)(2,1)S(1)} %get-tuple-element.31), channel_id=1, source_target_pairs={{0,2},{1,3},{2,0},{3,1},{4,6},{5,7},{6,4},{7,5},{8,10},{9,11},{10,... | collective-permute-start | bytes 688136 | tf_op jit(solution)/shard_map/ppermute | solution.py:40
  14.9 1.3 collective-permute-start.2
  16.2 2.8 %collective-permute-done.refs_1_ = bf16[128,896]{1,0:T(8,128)(2,1)S(1)} collective-permute-done((bf16[128,896]{1,0:T(8,128)(2,1)S(1)}, bf16[128,896]{1,0:T(8,128)(2,1)S(1)}, u32[]{:S(2)}, u32[]{:S(2)}) %collective-permute-start) | collective-permute-done | bytes 229408 | tf_op jit(solution)/shard_map/ppermute | solution.py:40
  19.0 6.1 %collective-permute-done.1.refs_2_ = bf16[128,896]{1,0:T(8,128)(2,1)S(1)} collective-permute-done((bf16[128,896]{1,0:T(8,128)(2,1)S(1)}, bf16[128,896]{1,0:T(8,128)(2,1)S(1)}, u32[]{:S(2)}, u32[]{:S(2)}) %collective-permute-start.1) | collective-permute-done | bytes 229408 | tf_op jit(solution)/shard_map/ppermute | solution.py:40
  25.1 1.2 collective-permute-start.7
  26.3 2.4 collective-permute-start.8
  28.7 1.7 collective-permute-start.9
  30.5 2.0 collective-permute-start.3
  32.6 5.4 %collective-permute-done.8.refs_2_ = bf16[128,768]{1,0:T(8,128)(2,1)S(1)} collective-permute-done((bf16[128,768]{1,0:T(8,128)(2,1)S(1)}, bf16[128,768]{1,0:T(8,128)(2,1)S(1)}, u32[]{:S(2)}, u32[]{:S(2)}) %collective-permute-start.8) | collective-permute-done | bytes 196640 | tf_op jit(solution)/shard_map/ppermute | solution.py:40
  38.0 2.0 collective-permute-start.10
  40.1 13.7 %collective-permute-done.3.refs_3_.refs_10_ = bf16[512,896]{1,0:T(8,128)(2,1)S(1)} collective-permute-done((bf16[512,896]{1,0:T(8,128)(2,1)S(1)}, bf16[512,896]{1,0:T(8,128)(2,1)S(1)}, u32[]{:S(2)}, u32[]{:S(2)}) %collective-permute-start.3) | collective-permute-done | bytes 917536 | tf_op jit(solution)/shard_map/ppermute | solution.py:40
  53.9 2.0 collective-permute-start.5
  55.9 0.9 slice.25
  57.1 13.6 %collective-permute-done.10.refs_8_.refs_15_ = bf16[512,768]{1,0:T(8,128)(2,1)S(1)} collective-permute-done((bf16[512,768]{1,0:T(8,128)(2,1)S(1)}, bf16[512,768]{1,0:T(8,128)(2,1)S(1)}, u32[]{:S(2)}, u32[]{:S(2)}) %collective-permute-start.10) | collective-permute-done | bytes 786464 | tf_op jit(solution)/shard_map/ppermute | solution.py:40
  70.7 0.8 slice.26
  71.5 1.9 collective-permute-start.12
  73.5 0.8 copy-done.19
  76.5 9.4 %collective-permute-done.12.refs_10_.refs_17_ = bf16[256,768]{1,0:T(8,128)(2,1)} collective-permute-done((bf16[256,768]{1,0:T(8,128)(2,1)}, bf16[256,768]{1,0:T(8,128)(2,1)}, u32[]{:S(2)}, u32[]{:S(2)}) %collective-permute-start.12) | collective-permute-done | bytes 393248 | tf_op jit(solution)/shard_map/ppermute | solution.py:40
  85.9 1.5 collective-permute-done.13.refs_11_.refs_18_
  87.5 0.7 copy-done.21
  88.1 29.7 %layer.2 = (bf16[1024,1024]{1,0:T(8,128)(2,1)}, bf16[4,128,256]{2,1,0:T(8,128)(2,1)}, bf16[1024,512]{1,0:T(8,128)(2,1)}) custom-call(s32[3]{0:T(128)} %pad_add_fusion.3.where.refs_0_, f32[1,16]{1,0:T(1,128)} %bias_ref.3, bf16[1024,2048]{1,0:T(8,128)(2,1)} %all-gather.2.cloned.1.call-done.refs_0_, f32[1,2048]{1,0:T(1,128)} %refs_8_.3, ...), custom_call_target="tpu_custom_call" | custom-call | flops 8589934592 | bytes 11018316 | tf_op jit(solution)/shard_map/layer/pallas_call | solution.py:59
  117.9 1.7 collective-permute-start.14
  119.6 1.3 collective-permute-start.15
  120.9 2.3 collective-permute-start.16
  123.2 3.0 %collective-permute-done.14.refs_2_ = bf16[4,128,256]{2,1,0:T(8,128)(2,1)S(1)} collective-permute-done((bf16[4,128,256]{2,1,0:T(8,128)(2,1)}, bf16[4,128,256]{2,1,0:T(8,128)(2,1)S(1)}, u32[]{:S(2)}, u32[]{:S(2)}) %collective-permute-start.14) | collective-permute-done | bytes 262176 | tf_op jit(solution)/shard_map/ppermute | solution.py:40
  126.2 2.7 %collective-permute-done.15.refs_3_ = bf16[4,128,256]{2,1,0:T(8,128)(2,1)S(1)} collective-permute-done((bf16[4,128,256]{2,1,0:T(8,128)(2,1)}, bf16[4,128,256]{2,1,0:T(8,128)(2,1)S(1)}, u32[]{:S(2)}, u32[]{:S(2)}) %collective-permute-start.15) | collective-permute-done | bytes 262176 | tf_op jit(solution)/shard_map/ppermute | solution.py:40
  128.9 2.7 %collective-permute-done.16.refs_4_ = bf16[4,128,256]{2,1,0:T(8,128)(2,1)S(1)} collective-permute-done((bf16[4,128,256]{2,1,0:T(8,128)(2,1)}, bf16[4,128,256]{2,1,0:T(8,128)(2,1)S(1)}, u32[]{:S(2)}, u32[]{:S(2)}) %collective-permute-start.16) | collective-permute-done | bytes 262176 | tf_op jit(solution)/shard_map/ppermute | solution.py:40
  131.6 1.6 copy-done.2
  133.2 1.2 copy-done.4
  134.4 0.9 copy-done.12
  135.3 3.0 %finish.1 = (bf16[1024,256]{1,0:T(8,128)(2,1)S(1)}, bf16[1024,256]{1,0:T(8,128)(2,1)S(1)}, f32[4,128,128]{2,1,0:T(8,128)S(1)}) custom-call(s32[3]{0:T(128)S(1)} %copy-done.15, bf16[4,128,256]{2,1,0:T(8,128)(2,1)S(1)} %copy-done.12, bf16[4,128,256]{2,1,0:T(8,128)(2,1)S(1)} %collective-permute-done.14.refs_2_, ...), custom_call_target="tpu_custom_call" | custom-call | bytes 4456972 | tf_op jit(solution)/shard_map/finish/pallas_call | solution.py:59
  138.3 1.6 collective-permute-start.21
  139.9 7.0 %collective-permute-done.17.refs_0_.refs_7_ = bf16[1024,256]{1,0:T(8,128)(2,1)S(1)} collective-permute-done((bf16[1024,256]{1,0:T(8,128)(2,1)S(1)}, bf16[1024,256]{1,0:T(8,128)(2,1)S(1)}, u32[]{:S(2)}, u32[]{:S(2)}) %collective-permute-start.17) | collective-permute-done | bytes 524320 | tf_op jit(solution)/shard_map/ppermute | solution.py:40
  146.9 3.0 %collective-permute-start.18 = (bf16[1024,256]{1,0:T(8,128)(2,1)S(1)}, bf16[1024,256]{1,0:T(8,128)(2,1)}, u32[]{:S(2)}, u32[]{:S(2)}) collective-permute-start(bf16[1024,256]{1,0:T(8,128)(2,1)S(1)} %collective-permute-done.17.refs_0_.refs_7_), channel_id=1, source_target_pairs={{0,1},{1,2},{2,3},{3,0},{4,5},{5,6},{6,7},{7,4},{8,9},{9,10},{10,1... | collective-permute-start | bytes 1572872 | tf_op jit(solution)/shard_map/ppermute | solution.py:40
  149.9 2.6 collective-permute-done.21.refs_4_.refs_8_
  152.6 1.0 collective-permute-start.23
  153.5 1.6 collective-permute-start.19
  155.6 7.5 %collective-permute-done.18.refs_1_ = bf16[1024,256]{1,0:T(8,128)(2,1)} collective-permute-done((bf16[1024,256]{1,0:T(8,128)(2,1)S(1)}, bf16[1024,256]{1,0:T(8,128)(2,1)}, u32[]{:S(2)}, u32[]{:S(2)}) %collective-permute-start.18) | collective-permute-done | bytes 524320 | tf_op jit(solution)/shard_map/ppermute | solution.py:40
  163.1 1.8 collective-permute-start.20
  164.9 3.6 %collective-permute-done.23.refs_6_ = bf16[1024,256]{1,0:T(8,128)(2,1)} collective-permute-done((bf16[1024,256]{1,0:T(8,128)(2,1)S(1)}, bf16[1024,256]{1,0:T(8,128)(2,1)}, u32[]{:S(2)}, u32[]{:S(2)}) %collective-permute-start.23) | collective-permute-done | bytes 524320 | tf_op jit(solution)/shard_map/ppermute | solution.py:40
  168.5 1.2 collective-permute-start.24
  171.0 8.7 %collective-permute-done.19.refs_2_ = bf16[1024,256]{1,0:T(8,128)(2,1)} collective-permute-done((bf16[1024,256]{1,0:T(8,128)(2,1)S(1)}, bf16[1024,256]{1,0:T(8,128)(2,1)}, u32[]{:S(2)}, u32[]{:S(2)}) %collective-permute-start.19) | collective-permute-done | bytes 524320 | tf_op jit(solution)/shard_map/ppermute | solution.py:40
  179.7 3.9 %collective-permute-done.20.refs_3_ = bf16[1024,256]{1,0:T(8,128)(2,1)} collective-permute-done((bf16[1024,256]{1,0:T(8,128)(2,1)}, bf16[1024,256]{1,0:T(8,128)(2,1)}, u32[]{:S(2)}, u32[]{:S(2)}) %collective-permute-start.20) | collective-permute-done | bytes 524320 | tf_op jit(solution)/shard_map/ppermute | solution.py:40
  183.7 5.7 %collective-permute-done.24.refs_7_ = bf16[1024,256]{1,0:T(8,128)(2,1)} collective-permute-done((bf16[1024,256]{1,0:T(8,128)(2,1)}, bf16[1024,256]{1,0:T(8,128)(2,1)}, u32[]{:S(2)}, u32[]{:S(2)}) %collective-permute-start.24) | collective-permute-done | bytes 524320 | tf_op jit(solution)/shard_map/ppermute | solution.py:40
  189.4 29.2 %layer.3 = (bf16[1024,1024]{1,0:T(8,128)(2,1)}, bf16[4,128,256]{2,1,0:T(8,128)(2,1)}) custom-call(s32[3]{0:T(128)} %pad_add_fusion.1.where.refs_0_, f32[1,16]{1,0:T(1,128)} %bias_ref.3, bf16[1024,256]{1,0:T(8,128)(2,1)} %copy-done.7, bf16[1024,256]{1,0:T(8,128)(2,1)} %collective-permute-done.18.refs_1_, bf16[1024,256]{1,0:T(8,128)(2,1)} %collective-permute-done.19.refs_2_, ...), custom_call_target="tpu_custom_call" | custom-call | flops 8589934592 | bytes 11018316 | tf_op jit(solution)/shard_map/layer/pallas_call | solution.py:59
  218.6 0.7 collective-permute-start.25
  219.4 2.0 collective-permute-start.26
  221.3 1.8 collective-permute-start.27
  223.1 5.0 %collective-permute-done.25.refs_2_ = bf16[4,128,256]{2,1,0:T(8,128)(2,1)S(1)} collective-permute-done((bf16[4,128,256]{2,1,0:T(8,128)(2,1)}, bf16[4,128,256]{2,1,0:T(8,128)(2,1)S(1)}, u32[]{:S(2)}, u32[]{:S(2)}) %collective-permute-start.25) | collective-permute-done | bytes 262176 | tf_op jit(solution)/shard_map/ppermute | solution.py:40
  228.1 2.2 collective-permute-done.26.refs_3_
  230.3 2.8 %collective-permute-done.27.refs_4_ = bf16[4,128,256]{2,1,0:T(8,128)(2,1)S(1)} collective-permute-done((bf16[4,128,256]{2,1,0:T(8,128)(2,1)}, bf16[4,128,256]{2,1,0:T(8,128)(2,1)S(1)}, u32[]{:S(2)}, u32[]{:S(2)}) %collective-permute-start.27) | collective-permute-done | bytes 262176 | tf_op jit(solution)/shard_map/ppermute | solution.py:40
  233.1 1.6 copy-done.1
  234.7 1.0 copy-done.8
  235.7 1.0 copy-done.10
  236.7 0.9 copy-done.11
  237.7 2.2 finish_last.1
  239.9 1.6 collective-permute-start.28
  242.1 2.1 collective-permute-start.30
  244.2 10.6 %collective-permute-done.28.refs_1_ = bf16[256,512]{1,0:T(8,128)(2,1)S(1)} collective-permute-done((bf16[256,512]{1,0:T(8,128)(2,1)S(1)}, bf16[256,512]{1,0:T(8,128)(2,1)S(1)}, u32[]{:S(2)}, u32[]{:S(2)}) %collective-permute-start.28) | collective-permute-done | bytes 262176 | tf_op jit(solution)/shard_map/ppermute | solution.py:40
  255.5 1.6 place.1
  (63 shorter events, 4.9 us)
Async XLA Ops:
  6.5 116.7 %copy-start = (f32[1,16,128,128]{3,2,1,0:T(8,128)S(1)}, f32[1,16,128,128]{3,2,1,0:T(8,128)}, u32[]{:S(2)}) copy-start(f32[1,16,128,128]{3,2,1,0:T(8,128)} %param.14) | copy-start | bytes 3145732
  6.5 80.9 %all-gather.2.cloned.1.call-start = ((), (), s32[]{:S(2)}) async-start(), calls=%async_computation | async-start | bytes 5242880 | tf_op jit(solution)/shard_map/all_gather | solution.py:359
  7.5 1.4 copy-start.3
  10.4 8.6 %collective-permute-start = (bf16[128,896]{1,0:T(8,128)(2,1)S(1)}, bf16[128,896]{1,0:T(8,128)(2,1)S(1)}, u32[]{:S(2)}, u32[]{:S(2)}) collective-permute-start(bf16[128,896]{1,0:T(8,128)(2,1)S(1)} %get-tuple-element.30), channel_id=1, source_target_pairs={{0,1},{1,2},{2,3},{3,0},{4,5},{5,6},{6,7},{7,4},{8,9},{9,10},{10,1... | collective-permute-start | bytes 688136 | tf_op jit(solution)/shard_map/ppermute | solution.py:40
  12.0 13.1 %collective-permute-start.1 = (bf16[128,896]{1,0:T(8,128)(2,1)S(1)}, bf16[128,896]{1,0:T(8,128)(2,1)S(1)}, u32[]{:S(2)}, u32[]{:S(2)}) collective-permute-start(bf16[128,896]{1,0:T(8,128)(2,1)S(1)} %get-tuple-element.31), channel_id=1, source_target_pairs={{0,2},{1,3},{2,0},{3,1},{4,6},{5,7},{6,4},{7,5},{8,10},{9,11},{10,... | collective-permute-start | bytes 688136 | tf_op jit(solution)/shard_map/ppermute | solution.py:40
  14.9 10.2 %collective-permute-start.2 = (bf16[128,896]{1,0:T(8,128)(2,1)S(1)}, bf16[128,896]{1,0:T(8,128)(2,1)S(1)}, u32[]{:S(2)}, u32[]{:S(2)}) collective-permute-start(bf16[128,896]{1,0:T(8,128)(2,1)S(1)} %get-tuple-element.32), channel_id=1, source_target_pairs={{0,3},{1,0},{2,1},{3,2},{4,7},{5,4},{6,5},{7,6},{8,11},{9,8},{10,9... | collective-permute-start | bytes 688136 | tf_op jit(solution)/shard_map/ppermute | solution.py:40
  25.1 7.5 %collective-permute-start.7 = (bf16[128,768]{1,0:T(8,128)(2,1)}, bf16[128,768]{1,0:T(8,128)(2,1)S(1)}, u32[]{:S(2)}, u32[]{:S(2)}) collective-permute-start(bf16[128,768]{1,0:T(8,128)(2,1)} %get-tuple-element.40), channel_id=1, source_target_pairs={{0,1},{1,2},{2,3},{3,0},{4,5},{5,6},{6,7},{7,4},{8,9},{9,10},{10,1... | collective-permute-start | bytes 589832 | tf_op jit(solution)/shard_map/ppermute | solution.py:40
  26.3 11.6 %collective-permute-start.8 = (bf16[128,768]{1,0:T(8,128)(2,1)S(1)}, bf16[128,768]{1,0:T(8,128)(2,1)S(1)}, u32[]{:S(2)}, u32[]{:S(2)}) collective-permute-start(bf16[128,768]{1,0:T(8,128)(2,1)S(1)} %get-tuple-element.41), channel_id=1, source_target_pairs={{0,2},{1,3},{2,0},{3,1},{4,6},{5,7},{6,4},{7,5},{8,10},{9,11},{10,... | collective-permute-start | bytes 589832 | tf_op jit(solution)/shard_map/ppermute | solution.py:40
  28.7 9.2 %collective-permute-start.9 = (bf16[128,768]{1,0:T(8,128)(2,1)S(1)}, bf16[128,768]{1,0:T(8,128)(2,1)S(1)}, u32[]{:S(2)}, u32[]{:S(2)}) collective-permute-start(bf16[128,768]{1,0:T(8,128)(2,1)S(1)} %get-tuple-element.42), channel_id=1, source_target_pairs={{0,3},{1,0},{2,1},{3,2},{4,7},{5,4},{6,5},{7,6},{8,11},{9,8},{10,9... | collective-permute-start | bytes 589832 | tf_op jit(solution)/shard_map/ppermute | solution.py:40
  30.5 41.0 %copy-start.5 = (bf16[512,896]{1,0:T(8,128)(2,1)}, bf16[512,896]{1,0:T(8,128)(2,1)S(1)}, u32[]{:S(2)}) copy-start(bf16[512,896]{1,0:T(8,128)(2,1)S(1)} %join.2.refs_2_.refs_9_) | copy-start | bytes 2752516
  30.5 23.4 %collective-permute-start.3 = (bf16[512,896]{1,0:T(8,128)(2,1)S(1)}, bf16[512,896]{1,0:T(8,128)(2,1)S(1)}, u32[]{:S(2)}, u32[]{:S(2)}) collective-permute-start(bf16[512,896]{1,0:T(8,128)(2,1)S(1)} %join.2.refs_2_.refs_9_), channel_id=1, source_target_pairs={{0,4},{4,8},{8,12},{12,0},{1,5},{5,9},{9,13},{13,1},{2,6},{6,10},{... | collective-permute-start | bytes 2752520 | tf_op jit(solution)/shard_map/ppermute | solution.py:40
  32.5 23.4 %collective-permute-start.4 = (bf16[512,896]{1,0:T(8,128)(2,1)S(1)}, bf16[512,896]{1,0:T(8,128)(2,1)S(1)}, u32[]{:S(2)}, u32[]{:S(2)}) collective-permute-start(bf16[512,896]{1,0:T(8,128)(2,1)S(1)} %join.2.refs_2_.refs_9_), channel_id=1, source_target_pairs={{0,12},{4,0},{8,4},{12,8},{1,13},{5,1},{9,5},{13,9},{2,14},{6,2},{... | collective-permute-start | bytes 2752520 | tf_op jit(solution)/shard_map/ppermute | solution.py:40
  38.0 49.4 %copy-start.6 = (bf16[512,768]{1,0:T(8,128)(2,1)}, bf16[512,768]{1,0:T(8,128)(2,1)S(1)}, u32[]{:S(2)}) copy-start(bf16[512,768]{1,0:T(8,128)(2,1)S(1)} %join.3.refs_7_.refs_14_) | copy-start | bytes 2359300
  38.0 36.5 %copy-start.20 = (s32[2,1]{0,1:T(1,128)S(1)}, s32[2,1]{0,1:T(1,128)}, u32[]{:S(2)}) copy-start(s32[2,1]{0,1:T(1,128)} %param.15) | copy-start | bytes 28
  38.0 32.7 %collective-permute-start.10 = (bf16[512,768]{1,0:T(8,128)(2,1)S(1)}, bf16[512,768]{1,0:T(8,128)(2,1)S(1)}, u32[]{:S(2)}, u32[]{:S(2)}) collective-permute-start(bf16[512,768]{1,0:T(8,128)(2,1)S(1)} %join.3.refs_7_.refs_14_), channel_id=1, source_target_pairs={{0,4},{4,8},{8,12},{12,0},{1,5},{5,9},{9,13},{13,1},{2,6},{6,10},{... | collective-permute-start | bytes 2359304 | tf_op jit(solution)/shard_map/ppermute | solution.py:40
  40.0 33.4 %collective-permute-start.11 = (bf16[512,768]{1,0:T(8,128)(2,1)S(1)}, bf16[512,768]{1,0:T(8,128)(2,1)S(1)}, u32[]{:S(2)}, u32[]{:S(2)}) collective-permute-start(bf16[512,768]{1,0:T(8,128)(2,1)S(1)} %join.3.refs_7_.refs_14_), channel_id=1, source_target_pairs={{0,12},{4,0},{8,4},{12,8},{1,13},{5,1},{9,5},{13,9},{2,14},{6,2},{... | collective-permute-start | bytes 2359304 | tf_op jit(solution)/shard_map/ppermute | solution.py:40
  53.8 19.6 %copy-start.16 = (bf16[512,896]{1,0:T(8,128)(2,1)}, bf16[512,896]{1,0:T(8,128)(2,1)S(1)}, u32[]{:S(2)}) copy-start(bf16[512,896]{1,0:T(8,128)(2,1)S(1)} %collective-permute-done.3.refs_3_.refs_10_) | copy-start | bytes 2752516
  53.9 33.5 %collective-permute-start.5 = (bf16[256,896]{1,0:T(8,128)(2,1)S(1)}, bf16[256,896]{1,0:T(8,128)(2,1)}, u32[]{:S(2)}, u32[]{:S(2)}) collective-permute-start(bf16[256,896]{1,0:T(8,128)(2,1)S(1)} %slice.24), channel_id=1, source_target_pairs={{0,4},{4,8},{8,12},{12,0},{1,5},{5,9},{9,13},{13,1},{2,6},{6,10},{... | collective-permute-start | bytes 1376264 | tf_op jit(solution)/shard_map/ppermute | solution.py:40
  55.9 17.6 %copy-start.17 = (bf16[512,896]{1,0:T(8,128)(2,1)}, bf16[512,896]{1,0:T(8,128)(2,1)S(1)}, u32[]{:S(2)}) copy-start(bf16[512,896]{1,0:T(8,128)(2,1)S(1)} %collective-permute-done.4.refs_4_.refs_11_) | copy-start | bytes 2752516
  56.8 30.6 %collective-permute-start.6 = (bf16[256,896]{1,0:T(8,128)(2,1)}, bf16[256,896]{1,0:T(8,128)(2,1)}, u32[]{:S(2)}, u32[]{:S(2)}) collective-permute-start(bf16[256,896]{1,0:T(8,128)(2,1)} %slice.25), channel_id=1, source_target_pairs={{0,12},{4,0},{8,4},{12,8},{1,13},{5,1},{9,5},{13,9},{2,14},{6,2},{... | collective-permute-start | bytes 1376264 | tf_op jit(solution)/shard_map/ppermute | solution.py:40
  70.7 2.8 %copy-start.18 = (bf16[512,768]{1,0:T(8,128)(2,1)}, bf16[512,768]{1,0:T(8,128)(2,1)S(1)}, u32[]{:S(2)}) copy-start(bf16[512,768]{1,0:T(8,128)(2,1)S(1)} %collective-permute-done.10.refs_8_.refs_15_) | copy-start | bytes 2359300
  71.5 14.4 %collective-permute-start.12 = (bf16[256,768]{1,0:T(8,128)(2,1)}, bf16[256,768]{1,0:T(8,128)(2,1)}, u32[]{:S(2)}, u32[]{:S(2)}) collective-permute-start(bf16[256,768]{1,0:T(8,128)(2,1)} %slice.26), channel_id=1, source_target_pairs={{0,4},{4,8},{8,12},{12,0},{1,5},{5,9},{9,13},{13,1},{2,6},{6,10},{... | collective-permute-start | bytes 1179656 | tf_op jit(solution)/shard_map/ppermute | solution.py:40
  73.4 0.9 copy-start.19
  74.3 13.1 %collective-permute-start.13 = (bf16[256,768]{1,0:T(8,128)(2,1)S(1)}, bf16[256,768]{1,0:T(8,128)(2,1)S(1)}, u32[]{:S(2)}, u32[]{:S(2)}) collective-permute-start(bf16[256,768]{1,0:T(8,128)(2,1)S(1)} %slice.27), channel_id=1, source_target_pairs={{0,12},{4,0},{8,4},{12,8},{1,13},{5,1},{9,5},{13,9},{2,14},{6,2},{... | collective-permute-start | bytes 1179656 | tf_op jit(solution)/shard_map/ppermute | solution.py:40
  76.5 55.1 %copy-start.13 = (f32[1,128]{1,0:T(1,128)S(1)}, f32[1,128]{1,0:T(1,128)}, u32[]{:S(2)}) copy-start(f32[1,128]{1,0:T(1,128)} %refs_9_.1) | copy-start | bytes 1540
  76.5 55.1 %copy-start.15 = (s32[3]{0:T(128)S(1)}, s32[3]{0:T(128)}, u32[]{:S(2)}) copy-start(s32[3]{0:T(128)} %pad_add_fusion.3.where.refs_0_) | copy-start | bytes 40
  87.4 0.7 copy-start.21
  117.9 8.4 %collective-permute-start.14 = (bf16[4,128,256]{2,1,0:T(8,128)(2,1)}, bf16[4,128,256]{2,1,0:T(8,128)(2,1)S(1)}, u32[]{:S(2)}, u32[]{:S(2)}) collective-permute-start(bf16[4,128,256]{2,1,0:T(8,128)(2,1)} %get-tuple-element.43.refs_1_), channel_id=1, source_target_pairs={{0,4},{4,8},{8,12},{12,0},{1,5},{5,9},{9,13},{13,1},{2,6},{6,10},{... | collective-permute-start | bytes 786440 | tf_op jit(solution)/shard_map/ppermute | solution.py:40
  119.6 9.4 %collective-permute-start.15 = (bf16[4,128,256]{2,1,0:T(8,128)(2,1)}, bf16[4,128,256]{2,1,0:T(8,128)(2,1)S(1)}, u32[]{:S(2)}, u32[]{:S(2)}) collective-permute-start(bf16[4,128,256]{2,1,0:T(8,128)(2,1)} %get-tuple-element.43.refs_1_), channel_id=1, source_target_pairs={{0,8},{4,12},{8,0},{12,4},{1,9},{5,13},{9,1},{13,5},{2,10},{6,14},... | collective-permute-start | bytes 786440 | tf_op jit(solution)/shard_map/ppermute | solution.py:40
  120.9 10.7 %collective-permute-start.16 = (bf16[4,128,256]{2,1,0:T(8,128)(2,1)}, bf16[4,128,256]{2,1,0:T(8,128)(2,1)S(1)}, u32[]{:S(2)}, u32[]{:S(2)}) collective-permute-start(bf16[4,128,256]{2,1,0:T(8,128)(2,1)} %get-tuple-element.43.refs_1_), channel_id=1, source_target_pairs={{0,12},{4,0},{8,4},{12,8},{1,13},{5,1},{9,5},{13,9},{2,14},{6,2},{... | collective-permute-start | bytes 786440 | tf_op jit(solution)/shard_map/ppermute | solution.py:40
  131.6 1.6 copy-start.2
  133.2 1.2 copy-start.4
  134.4 0.9 copy-start.12
  138.3 8.6 %collective-permute-start.17 = (bf16[1024,256]{1,0:T(8,128)(2,1)S(1)}, bf16[1024,256]{1,0:T(8,128)(2,1)S(1)}, u32[]{:S(2)}, u32[]{:S(2)}) collective-permute-start(bf16[1024,256]{1,0:T(8,128)(2,1)S(1)} %get-tuple-element.46), channel_id=1, source_target_pairs={{0,16},{16,32},{32,48},{48,64},{64,80},{80,96},{96,112},{112,0},{1... | collective-permute-start | bytes 1572872 | tf_op jit(solution)/shard_map/ppermute | solution.py:40
  138.3 14.2 %collective-permute-start.21 = (bf16[1024,256]{1,0:T(8,128)(2,1)S(1)}, bf16[1024,256]{1,0:T(8,128)(2,1)S(1)}, u32[]{:S(2)}, u32[]{:S(2)}) collective-permute-start(bf16[1024,256]{1,0:T(8,128)(2,1)S(1)} %get-tuple-element.47), channel_id=1, source_target_pairs={{0,16},{16,32},{32,48},{48,64},{64,80},{80,96},{96,112},{112,0},{1... | collective-permute-start | bytes 1572872 | tf_op jit(solution)/shard_map/ppermute | solution.py:40
  146.9 42.4 %copy-start.7 = (bf16[1024,256]{1,0:T(8,128)(2,1)}, bf16[1024,256]{1,0:T(8,128)(2,1)S(1)}, u32[]{:S(2)}) copy-start(bf16[1024,256]{1,0:T(8,128)(2,1)S(1)} %collective-permute-done.17.refs_0_.refs_7_) | copy-start | bytes 1572868
  146.9 16.2 %collective-permute-start.18 = (bf16[1024,256]{1,0:T(8,128)(2,1)S(1)}, bf16[1024,256]{1,0:T(8,128)(2,1)}, u32[]{:S(2)}, u32[]{:S(2)}) collective-permute-start(bf16[1024,256]{1,0:T(8,128)(2,1)S(1)} %collective-permute-done.17.refs_0_.refs_7_), channel_id=1, source_target_pairs={{0,1},{1,2},{2,3},{3,0},{4,5},{5,6},{6,7},{7,4},{8,9},{9,10},{10,1... | collective-permute-start | bytes 1572872 | tf_op jit(solution)/shard_map/ppermute | solution.py:40
  152.6 36.8 %copy-start.9 = (bf16[1024,256]{1,0:T(8,128)(2,1)}, bf16[1024,256]{1,0:T(8,128)(2,1)S(1)}, u32[]{:S(2)}) copy-start(bf16[1024,256]{1,0:T(8,128)(2,1)S(1)} %collective-permute-done.21.refs_4_.refs_8_) | copy-start | bytes 1572868
  152.6 16.0 %collective-permute-start.23 = (bf16[1024,256]{1,0:T(8,128)(2,1)S(1)}, bf16[1024,256]{1,0:T(8,128)(2,1)}, u32[]{:S(2)}, u32[]{:S(2)}) collective-permute-start(bf16[1024,256]{1,0:T(8,128)(2,1)S(1)} %collective-permute-done.21.refs_4_.refs_8_), channel_id=1, source_target_pairs={{0,3},{1,0},{2,1},{3,2},{4,7},{5,4},{6,5},{7,6},{8,11},{9,8},{10,9... | collective-permute-start | bytes 1572872 | tf_op jit(solution)/shard_map/ppermute | solution.py:40
  153.5 26.2 %collective-permute-start.19 = (bf16[1024,256]{1,0:T(8,128)(2,1)S(1)}, bf16[1024,256]{1,0:T(8,128)(2,1)}, u32[]{:S(2)}, u32[]{:S(2)}) collective-permute-start(bf16[1024,256]{1,0:T(8,128)(2,1)S(1)} %collective-permute-done.17.refs_0_.refs_7_), channel_id=1, source_target_pairs={{0,3},{1,0},{2,1},{3,2},{4,7},{5,4},{6,5},{7,6},{8,11},{9,8},{10,9... | collective-permute-start | bytes 1572872 | tf_op jit(solution)/shard_map/ppermute | solution.py:40
  155.1 24.6 %collective-permute-start.22 = (bf16[1024,256]{1,0:T(8,128)(2,1)S(1)}, bf16[1024,256]{1,0:T(8,128)(2,1)}, u32[]{:S(2)}, u32[]{:S(2)}) collective-permute-start(bf16[1024,256]{1,0:T(8,128)(2,1)S(1)} %collective-permute-done.21.refs_4_.refs_8_), channel_id=1, source_target_pairs={{0,1},{1,2},{2,3},{3,0},{4,5},{5,6},{6,7},{7,4},{8,9},{9,10},{10,1... | collective-permute-start | bytes 1572872 | tf_op jit(solution)/shard_map/ppermute | solution.py:40
  163.1 20.6 %collective-permute-start.20 = (bf16[1024,256]{1,0:T(8,128)(2,1)}, bf16[1024,256]{1,0:T(8,128)(2,1)}, u32[]{:S(2)}, u32[]{:S(2)}) collective-permute-start(bf16[1024,256]{1,0:T(8,128)(2,1)} %collective-permute-done.18.refs_1_), channel_id=1, source_target_pairs={{0,1},{1,2},{2,3},{3,0},{4,5},{5,6},{6,7},{7,4},{8,9},{9,10},{10,1... | collective-permute-start | bytes 1572872 | tf_op jit(solution)/shard_map/ppermute | solution.py:40
  168.5 20.8 %collective-permute-start.24 = (bf16[1024,256]{1,0:T(8,128)(2,1)}, bf16[1024,256]{1,0:T(8,128)(2,1)}, u32[]{:S(2)}, u32[]{:S(2)}) collective-permute-start(bf16[1024,256]{1,0:T(8,128)(2,1)} %collective-permute-done.23.refs_6_), channel_id=1, source_target_pairs={{0,3},{1,0},{2,1},{3,2},{4,7},{5,4},{6,5},{7,6},{8,11},{9,8},{10,9... | collective-permute-start | bytes 1572872 | tf_op jit(solution)/shard_map/ppermute | solution.py:40
  171.0 62.0 %copy-start.14 = (s32[3]{0:T(128)S(1)}, s32[3]{0:T(128)}, u32[]{:S(2)}) copy-start(s32[3]{0:T(128)} %pad_add_fusion.1.where.refs_0_) | copy-start | bytes 40
  218.6 9.5 %collective-permute-start.25 = (bf16[4,128,256]{2,1,0:T(8,128)(2,1)}, bf16[4,128,256]{2,1,0:T(8,128)(2,1)S(1)}, u32[]{:S(2)}, u32[]{:S(2)}) collective-permute-start(bf16[4,128,256]{2,1,0:T(8,128)(2,1)} %get-tuple-element.48.refs_1_), channel_id=1, source_target_pairs={{0,4},{4,8},{8,12},{12,0},{1,5},{5,9},{9,13},{13,1},{2,6},{6,10},{... | collective-permute-start | bytes 786440 | tf_op jit(solution)/shard_map/ppermute | solution.py:40
  219.4 10.9 %collective-permute-start.26 = (bf16[4,128,256]{2,1,0:T(8,128)(2,1)}, bf16[4,128,256]{2,1,0:T(8,128)(2,1)S(1)}, u32[]{:S(2)}, u32[]{:S(2)}) collective-permute-start(bf16[4,128,256]{2,1,0:T(8,128)(2,1)} %get-tuple-element.48.refs_1_), channel_id=1, source_target_pairs={{0,8},{4,12},{8,0},{12,4},{1,9},{5,13},{9,1},{13,5},{2,10},{6,14},... | collective-permute-start | bytes 786440 | tf_op jit(solution)/shard_map/ppermute | solution.py:40
  221.3 11.7 %collective-permute-start.27 = (bf16[4,128,256]{2,1,0:T(8,128)(2,1)}, bf16[4,128,256]{2,1,0:T(8,128)(2,1)S(1)}, u32[]{:S(2)}, u32[]{:S(2)}) collective-permute-start(bf16[4,128,256]{2,1,0:T(8,128)(2,1)} %get-tuple-element.48.refs_1_), channel_id=1, source_target_pairs={{0,12},{4,0},{8,4},{12,8},{1,13},{5,1},{9,5},{13,9},{2,14},{6,2},{... | collective-permute-start | bytes 786440 | tf_op jit(solution)/shard_map/ppermute | solution.py:40
  233.1 1.6 copy-start.1
  234.7 1.0 copy-start.8
  235.7 1.0 copy-start.10
  236.7 0.9 copy-start.11
  239.9 15.0 %collective-permute-start.28 = (bf16[256,512]{1,0:T(8,128)(2,1)S(1)}, bf16[256,512]{1,0:T(8,128)(2,1)S(1)}, u32[]{:S(2)}, u32[]{:S(2)}) collective-permute-start(bf16[256,512]{1,0:T(8,128)(2,1)S(1)} %get-tuple-element.52), channel_id=1, source_target_pairs={{0,1},{1,2},{2,3},{3,0},{4,5},{5,6},{6,7},{7,4},{8,9},{9,10},{10,1... | collective-permute-start | bytes 786440 | tf_op jit(solution)/shard_map/ppermute | solution.py:40
  241.5 13.4 %collective-permute-start.29 = (bf16[256,512]{1,0:T(8,128)(2,1)S(1)}, bf16[256,512]{1,0:T(8,128)(2,1)S(1)}, u32[]{:S(2)}, u32[]{:S(2)}) collective-permute-start(bf16[256,512]{1,0:T(8,128)(2,1)S(1)} %get-tuple-element.53), channel_id=1, source_target_pairs={{0,2},{1,3},{2,0},{3,1},{4,6},{5,7},{6,4},{7,5},{8,10},{9,11},{10,... | collective-permute-start | bytes 786440 | tf_op jit(solution)/shard_map/ppermute | solution.py:40
  242.1 13.4 %collective-permute-start.30 = (bf16[256,512]{1,0:T(8,128)(2,1)S(1)}, bf16[256,512]{1,0:T(8,128)(2,1)S(1)}, u32[]{:S(2)}, u32[]{:S(2)}) collective-permute-start(bf16[256,512]{1,0:T(8,128)(2,1)S(1)} %get-tuple-element.54), channel_id=1, source_target_pairs={{0,3},{1,0},{2,1},{3,2},{4,7},{5,4},{6,5},{7,6},{8,11},{9,8},{10,9... | collective-permute-start | bytes 786440 | tf_op jit(solution)/shard_map/ppermute | solution.py:40
Sparse Core Ops, SparseCore 0:
  25.2 49.6 all-gather.1
where the time goes:
time: 264 us
  waiting for transfers between devices  121 us (46%)
  Pallas kernels  67.3 us (25%)
  starting transfers between devices  44.6 us (17%)
  between operations  14.9 us (6%)
  local copies, waits for them, and re-layouts  14.7 us (6%)
    ppermute x31, waiting for transfers between devices, shift(): lax.ppermute(value, axis, [(i, (i + by) % count) for i in range(count)])  121 us
    pallas_call x8, Pallas kernels, call(): pl.pallas_call(kernel, out_shape=outs, in_specs=ins, out_specs=jax.tree.m...  67.3 us
    ppermute x31, starting transfers between devices, shift(): lax.ppermute(value, axis, [(i, (i + by) % count) for i in range(count)])  44.6 us
    unnamed x45, local copies, waits for them, and re-layouts  12.2 us
  transfers between devices with their start and end apart: 32, of which 22 were waited for; matrix products, arithmetic and copies ran while one was open for 1% of the time, Pallas kernels for 0%

commit v1 on v0

--- a/solution.py
+++ b/solution.py
@@ -47,6 +47,13 @@
     return value, left, right, across
 
 
+def halves_around(value, axis, *others):
+    left, right = shift(value, axis, 1), shift(value, axis, -1)
+    half = value.shape[0] // 2
+    passed = after((left, right), *others) if others else (left, right)
+    return value, left, right, shift(passed[0][:half], axis, 1), shift(passed[1][half:], axis, -1)
+
+
 def after(value, *others):
     return lax.optimization_barrier((value, *others))[0]
 
@@ -92,7 +99,7 @@
 
 
 def layer_kernel(tick, where, bias_ref, *refs):
-    count = 1 if tick == 0 else SIDE * len(GROUPS)
+    count = 5 if tick == 0 else SIDE * len(GROUPS)
     sources, refs = refs[:count], refs[count:]
     gain_ref, refs = refs[0], refs[1:]
     w_sources, refs = refs[: 5 * len(GROUPS)], refs[5 * len(GROUPS) :]
@@ -101,25 +108,25 @@
     x_ref, w0_ref, w1_ref, normed_ref, beta_ref, qkv_ref, state_ref, mask_ref, x_sems, w_sems = refs
     arrivals = []
     for at, ref in enumerate(sources):
-        step = STEPS[at % SIDE]
+        step = (STEPS + STEPS[-1:])[at] if tick == 0 else STEPS[at % SIDE]
         base = lax.rem(where[1] + step + SIDE, SIDE)
         if tick == 0:
-            target = x_ref
+            size = ref.shape[0]
+            target = x_ref.at[pl.ds(pl.multiple_of(base * 256 + (size if at == 4 else 0), size), size)]
         else:
             heads = GROUPS[at // SIDE]
             base = pl.multiple_of(base * (OWN * HD) + heads[0] * HD, HD)
             target = x_ref.at[:, pl.ds(base, len(heads) * HD)]
         arrivals.append(pltpu.make_async_copy(ref, target, x_sems.at[at]))
         arrivals[-1].start()
+    for copy in arrivals:
+        copy.wait()
     w_arrivals = []
     for at, ref in enumerate(w_sources):
         start = (0, 512, 1024, 1536, 1792)[at % 5]
         target = (w0_ref, w1_ref)[at // 5].at[start : start + ref.shape[0]]
         w_arrivals.append(pltpu.make_async_copy(ref, target, w_sems.at[at]))
         w_arrivals[-1].start()
-
-    for copy in arrivals:
-        copy.wait()
 
     def normalize(i, carry):
         rows = pl.ds(pl.multiple_of(i * TILE, TILE), TILE)
@@ -250,7 +257,12 @@
         m_ref[h] = state_ref[h].astype(BF)
 
 
-def finish_kernel(nh, split, where, m0, m1, m2, m3, s_ref, p_ref, x_refs, gain_ref, out_refs, final_ref, maps_ref):
+def finish_kernel(nh, split, where, m0, m1, m2, m3, s_ref, p_hbm, x_hbm, gain_ref, out_refs, final_ref, maps_ref, p_ref, x_ref, sems):
+    sources = (p_hbm, *x_hbm)
+    targets = (p_ref, *(x_ref.at[:, at * x_hbm[0].shape[1] : (at + 1) * x_hbm[0].shape[1]] for at in range(len(x_hbm))))
+    copies = [pltpu.make_async_copy(a, b, sems.at[at]) for at, (a, b) in enumerate(zip(sources, targets))]
+    for copy in copies:
+        copy.start()
     for s, ref in enumerate((m0, m1, m2, m3)):
         maps_ref[lax.rem(where[0] - s + SIDE, SIDE)] = ref[...]
     states = [s_ref[h] for h in range(nh)]
@@ -269,6 +281,8 @@
         for h in range(nh):
             final_ref[h] = states[h]
     entries = [first.astype(BF) for first in firsts]
+    for copy in copies:
+        copy.wait()
 
     def finish(rows, outs, out_rows):
         for h in range(nh):
@@ -276,9 +290,7 @@
             pb = p_ref[rows, h * 2 * HD + HD : (h + 1) * 2 * HD]
             o = dot(pa, entries[h]) + pb.astype(F32)
             o = o * lax.rsqrt(jnp.mean(o * o, axis=-1, keepdims=True) + 1e-05) * gain_ref[...]
-            x_ref = x_refs[h * len(x_refs) // nh]
-            at = h % (nh // len(x_refs)) * HD
-            x = x_ref[rows, at : at + HD].astype(F32)
+            x = x_ref[rows, h * HD : (h + 1) * HD].astype(F32)
             at = h % (nh // len(outs)) * HD
             outs[h * len(outs) // nh][out_rows, at : at + HD] = (x + o).astype(BF)
 
@@ -301,7 +313,7 @@
 
 
 def finish_last_kernel(nh, *refs):
-    finish_kernel(nh, True, *refs[:7], refs[7:9], refs[9], refs[10:14], None, refs[14])
+    finish_kernel(nh, True, *refs[:7], refs[7:9], refs[9], refs[10:14], None, *refs[14:])
 
 
 def pack_kernel(where, w_ref, wb_ref, *out_refs):
@@ -342,21 +354,18 @@
     widths = (width + HD, width)
     packs = [struct((HD, wide)) for wide in widths for _ in range(SIDE)]
     packed = call(pack_kernel, "pack", packs, [SM, VM, VM], (here, w_qkv[0], w_beta[0]))
-    sent = []
+    weights = []
     for g in range(len(GROUPS)):
         mine = packed[g * SIDE : g * SIDE + SIDE]
-        if sent:
-            mine = after(tuple(mine), *sent[-1][1:])
-        sent.append([mine[0]] + [shift(mine[s], "y", s) for s in range(1, SIDE)])
-    weights = []
-    for g in range(len(GROUPS)):
-        joined = call(join_kernel, "join", [struct((SIDE * HD, widths[g]))], [VM] * SIDE, tuple(sent[g]))[0]
-        left, right = shift(joined, "z", 1), shift(joined, "z", -1)
-        half = joined.shape[0] // 2
-        weights.append((joined, left, right, shift(left[:half], "z", 1), shift(right[half:], "z", -1)))
+        if weights:
+            mine = after(tuple(mine), *first[1:])
+        got = [mine[0]] + [shift(mine[s], "y", s) for s in range(1, SIDE)]
+        first = first if weights else got
+        joined = call(join_kernel, "join", [struct((SIDE * HD, widths[g]))], [VM] * SIDE, tuple(got))[0]
+        weights.append(halves_around(joined, "z", *(weights[-1][3:5] if weights else ())))
     flat = [piece for pieces in weights for piece in pieces]
-    x = after(residual[0], *sent[0][1:])
-    pieces = [lax.all_gather(x, "y", axis=0, tiled=True)]
+    x = after(residual[0], *weights[0][1:3], *got[1:])
+    pieces = halves_around(x, "y", *weights[1][1:3])
     states = lax.dynamic_slice_in_dim(state_in[0], y * OWN, OWN, axis=0)
 
     for tick in range(TICKS):
@@ -387,27 +396,34 @@
             vmem=60 << 20,
         )
         maps = [m] + [shift(m, "z", s) for s in range(1, SIDE)]
+        finish_scratch = [
+            pltpu.VMEM((SIDE, OWN, HD, 2 * HD), BF),
+            pltpu.VMEM((ROWS, OWN * 2 * HD), BF),
+            pltpu.VMEM((ROWS, OWN * HD), BF),
+        ]
         if tick + 1 < TICKS:
             pieces = []
             *outs, states = call(
                 functools.partial(finish_first_kernel, OWN),
                 "finish",
                 [struct((ROWS, OWN * HD // len(GROUPS)))] * len(GROUPS) + [struct((OWN, HD, HD), F32)],
-                [SM] + [VM] * 8,
+                [SM] + [VM] * 5 + [HBM] * 2 + [VM],
                 (where, *maps, states, p, rest[0], out_gain),
-                scratch=[pltpu.VMEM((SIDE, OWN, HD, 2 * HD), BF)],
+                scratch=finish_scratch + [pltpu.SemaphoreType.DMA((2,))],
+                vmem=60 << 20,
             )
-            moved = [shift(out, "section", 1, lax.axis_size("section")) for out in outs]
-            for g in range(len(GROUPS)):
-                pieces.extend(around(moved[g], "y", g == 0))
+            sections = lax.axis_size("section")
+            pieces.extend(around(shift(outs[0], "section", 1, sections), "y", True))
+            pieces.extend(shift(piece, "section", 1, sections) for piece in around(outs[1], "y", False))
         else:
             outs = call(
                 functools.partial(finish_last_kernel, OWN),
                 "finish_last",
                 [struct((256, OWN * HD))] * SIDE,
-                [SM] + [VM] * 9,
+                [SM] + [VM] * 5 + [HBM] * 3 + [VM],
                 (where, *maps, states, p, pieces[0], pieces[SIDE], out_gain),
-                scratch=[pltpu.VMEM((SIDE, OWN, HD, 2 * HD), BF)],
+                scratch=finish_scratch + [pltpu.SemaphoreType.DMA((3,))],
+                vmem=60 << 20,
             )
     outs = [outs[0]] + [shift(outs[s], "y", s) for s in range(1, SIDE)]
     out = call(place_kernel, "place", [struct((256, D))], [SM] + [VM] * SIDE, (here, *outs))[0]

time: 264 us -> 246 us (0.932)
  between operations: 14.9 us -> 1.69 us
  local copies, waits for them, and re-layouts: 14.7 us -> 7.09 us
  waiting for transfers between devices: 121 us -> 114 us
  starting transfers between devices: 44.6 us -> 51.5 us
    ppermute x31 -> x38, waiting for transfers between devices: 121 us -> 114 us  [shift(): lax.ppermute(value, axis, [(i, (i + by) % count) for i in range(count)])]
    ppermute x31 -> x38, starting transfers between devices: 44.6 us -> 51.5 us  [shift(): lax.ppermute(value, axis, [(i, (i + by) % count) for i in range(count)])]
    unnamed x45 -> x51, local copies, waits for them, and re-layouts: 12.2 us -> 5.48 us
  transfers between devices with their start and end apart: 32 -> 38, of which waited for: 22 -> 26; matrix products, arithmetic and copies ran while one was open for 1% -> 1% of each run, Pallas kernels for 0% -> 0%
where the time goes in v1:
time: 246 us; the launch traced here: 245 us
  waiting for transfers between devices  114 us (46%)
  Pallas kernels  69.4 us (28%)
  starting transfers between devices  51.5 us (21%)
  local copies, waits for them, and re-layouts  7.09 us (3%)
    ppermute x38, waiting for transfers between devices, shift(): lax.ppermute(value, axis, [(i, (i + by) % count) for i in range(count)])  114 us
    pallas_call x8, Pallas kernels, call(): pl.pallas_call(kernel, out_shape=outs, in_specs=ins, out_specs=jax.tree.m...  69.4 us
    ppermute x38, starting transfers between devices, shift(): lax.ppermute(value, axis, [(i, (i + by) % count) for i in range(count)])  51.5 us
    unnamed x51, local copies, waits for them, and re-layouts  5.48 us
  transfers between devices with their start and end apart: 38, of which 26 were waited for; matrix products, arithmetic and copies ran while one was open for 1% of the time, Pallas kernels for 0%

profile of v1, /device:TPU:34, one launch (start us, length us, event | category | flops | bytes accessed | tf_op | source)
XLA Modules:
  0.0 244.8 jit_solution(13599509436750740585)
XLA Ops:
  0.0 0.9 copy.9
  1.0 1.4 copy-done.1
  2.4 0.9 pack.1
  3.3 1.6 collective-permute-start
  5.0 2.9 %collective-permute-start.1 = (bf16[128,896]{1,0:T(8,128)(2,1)S(1)}, bf16[128,896]{1,0:T(8,128)(2,1)S(1)}, u32[]{:S(2)}, u32[]{:S(2)}) collective-permute-start(bf16[128,896]{1,0:T(8,128)(2,1)S(1)} %get-tuple-element.36), channel_id=1, source_target_pairs={{0,2},{1,3},{2,0},{3,1},{4,6},{5,7},{6,4},{7,5},{8,10},{9,11},{10,... | collective-permute-start | bytes 688136 | tf_op jit(solution)/shard_map/ppermute | solution.py:40
  7.9 1.3 collective-permute-start.2
  9.2 2.8 %collective-permute-done.refs_1_ = bf16[128,896]{1,0:T(8,128)(2,1)S(1)} collective-permute-done((bf16[128,896]{1,0:T(8,128)(2,1)S(1)}, bf16[128,896]{1,0:T(8,128)(2,1)S(1)}, u32[]{:S(2)}, u32[]{:S(2)}) %collective-permute-start) | collective-permute-done | bytes 229408 | tf_op jit(solution)/shard_map/ppermute | solution.py:40
  12.0 6.1 %collective-permute-done.1.refs_2_ = bf16[128,896]{1,0:T(8,128)(2,1)S(1)} collective-permute-done((bf16[128,896]{1,0:T(8,128)(2,1)S(1)}, bf16[128,896]{1,0:T(8,128)(2,1)S(1)}, u32[]{:S(2)}, u32[]{:S(2)}) %collective-permute-start.1) | collective-permute-done | bytes 229408 | tf_op jit(solution)/shard_map/ppermute | solution.py:40
  18.2 2.0 collective-permute-start.3
  20.3 1.2 collective-permute-start.5
  21.5 2.4 collective-permute-start.6
  23.9 1.6 collective-permute-start.7
  25.5 1.9 collective-permute-done.5.refs_1_
  27.4 5.1 %collective-permute-done.6.refs_2_ = bf16[128,768]{1,0:T(8,128)(2,1)S(1)} collective-permute-done((bf16[128,768]{1,0:T(8,128)(2,1)S(1)}, bf16[128,768]{1,0:T(8,128)(2,1)S(1)}, u32[]{:S(2)}, u32[]{:S(2)}) %collective-permute-start.6) | collective-permute-done | bytes 196640 | tf_op jit(solution)/shard_map/ppermute | solution.py:40
  32.6 1.8 collective-permute-start.10
  34.4 7.1 %collective-permute-done.3.refs_7_.refs_10_ = bf16[512,896]{1,0:T(8,128)(2,1)S(1)} collective-permute-done((bf16[512,896]{1,0:T(8,128)(2,1)S(1)}, bf16[512,896]{1,0:T(8,128)(2,1)S(1)}, u32[]{:S(2)}, u32[]{:S(2)}) %collective-permute-start.3) | collective-permute-done | bytes 917536 | tf_op jit(solution)/shard_map/ppermute | solution.py:40
  41.6 1.3 collective-permute-start.8
  42.9 2.0 collective-permute-start.9
  44.9 2.1 collective-permute-start.11
  47.2 11.2 %collective-permute-done.10.refs_12_.refs_15_ = bf16[512,768]{1,0:T(8,128)(2,1)S(1)} collective-permute-done((bf16[512,768]{1,0:T(8,128)(2,1)S(1)}, bf16[512,768]{1,0:T(8,128)(2,1)S(1)}, u32[]{:S(2)}, u32[]{:S(2)}) %collective-permute-start.10) | collective-permute-done | bytes 786464 | tf_op jit(solution)/shard_map/ppermute | solution.py:40
  58.4 2.1 collective-permute-start.15
  60.5 4.8 %collective-permute-done.11.refs_13_.refs_16_ = bf16[512,768]{1,0:T(8,128)(2,1)S(1)} collective-permute-done((bf16[512,768]{1,0:T(8,128)(2,1)S(1)}, bf16[512,768]{1,0:T(8,128)(2,1)S(1)}, u32[]{:S(2)}, u32[]{:S(2)}) %collective-permute-start.11) | collective-permute-done | bytes 786464 | tf_op jit(solution)/shard_map/ppermute | solution.py:40
  65.3 1.1 collective-permute-done.8.refs_1_
  66.6 1.2 collective-permute-start.12
  67.8 2.2 collective-permute-start.13
  70.0 2.3 collective-permute-done.15.refs_10_.refs_13_
  72.3 1.8 collective-permute-start.16
  76.7 3.9 %collective-permute-done.16.refs_14_.refs_17_ = bf16[256,768]{1,0:T(8,128)(2,1)} collective-permute-done((bf16[256,768]{1,0:T(8,128)(2,1)S(1)}, bf16[256,768]{1,0:T(8,128)(2,1)}, u32[]{:S(2)}, u32[]{:S(2)}) %collective-permute-start.16) | collective-permute-done | bytes 393248 | tf_op jit(solution)/shard_map/ppermute | solution.py:40
  80.7 2.9 %collective-permute-done.17.refs_15_.refs_18_ = bf16[256,768]{1,0:T(8,128)(2,1)S(1)} collective-permute-done((bf16[256,768]{1,0:T(8,128)(2,1)S(1)}, bf16[256,768]{1,0:T(8,128)(2,1)S(1)}, u32[]{:S(2)}, u32[]{:S(2)}) %collective-permute-start.17) | collective-permute-done | bytes 393248 | tf_op jit(solution)/shard_map/ppermute | solution.py:40
  83.6 0.8 copy-done.24
  84.4 28.4 %layer.2 = (bf16[1024,1024]{1,0:T(8,128)(2,1)}, bf16[4,128,256]{2,1,0:T(8,128)(2,1)}, bf16[1024,512]{1,0:T(8,128)(2,1)}) custom-call(s32[3]{0:T(128)} %pad_add_fusion.3.where.refs_0_, f32[1,16]{1,0:T(1,128)} %bias_ref.3, bf16[256,2048]{1,0:T(8,128)(2,1)} %bitcast.14, bf16[256,2048]{1,0:T(8,128)(2,1)} %copy-done.13, bf16[256,2048]{1,0:T(8,128)(2,1)} %copy-done.14, ...), custom_call_target="tpu_custom_call" | custom-call | flops 8589934592 | bytes 11018316 | tf_op jit(solution)/shard_map/layer/pallas_call | solution.py:66
  112.7 1.8 collective-permute-start.18
  114.5 1.4 collective-permute-start.19
  115.9 2.5 %collective-permute-start.20 = (bf16[4,128,256]{2,1,0:T(8,128)(2,1)}, bf16[4,128,256]{2,1,0:T(8,128)(2,1)S(1)}, u32[]{:S(2)}, u32[]{:S(2)}) collective-permute-start(bf16[4,128,256]{2,1,0:T(8,128)(2,1)} %get-tuple-element.51.refs_1_), channel_id=1, source_target_pairs={{0,12},{4,0},{8,4},{12,8},{1,13},{5,1},{9,5},{13,9},{2,14},{6,2},{... | collective-permute-start | bytes 786440 | tf_op jit(solution)/shard_map/ppermute | solution.py:40
  118.4 0.7 dynamic-slice_bitcast_fusion.refs_5_
  119.2 1.6 collective-permute-done.18.refs_2_
  120.8 2.4 collective-permute-done.19.refs_3_
  123.2 2.7 %collective-permute-done.20.refs_4_ = bf16[4,128,256]{2,1,0:T(8,128)(2,1)S(1)} collective-permute-done((bf16[4,128,256]{2,1,0:T(8,128)(2,1)}, bf16[4,128,256]{2,1,0:T(8,128)(2,1)S(1)}, u32[]{:S(2)}, u32[]{:S(2)}) %collective-permute-start.20) | collective-permute-done | bytes 262176 | tf_op jit(solution)/shard_map/ppermute | solution.py:40
  125.9 0.7 copy-done.9
  126.6 5.7 %finish.1 = (bf16[1024,256]{1,0:T(8,128)(2,1)}, bf16[1024,256]{1,0:T(8,128)(2,1)}, f32[4,128,128]{2,1,0:T(8,128)}) custom-call(s32[3]{0:T(128)} %pad_add_fusion.3.where.refs_0_, bf16[4,128,256]{2,1,0:T(8,128)(2,1)} %get-tuple-element.51.refs_1_, bf16[4,128,256]{2,1,0:T(8,128)(2,1)} %copy-done.7, bf16[4,128,256]{2,1,0:T(8,128)(2,1)} %copy-done.8, ...), custom_call_target="tpu_custom_call" | custom-call | bytes 4456972 | tf_op jit(solution)/shard_map/finish/pallas_call | solution.py:66
  132.3 2.8 %collective-permute-start.28 = (bf16[1024,256]{1,0:T(8,128)(2,1)}, bf16[1024,256]{1,0:T(8,128)(2,1)S(1)}, u32[]{:S(2)}, u32[]{:S(2)}) collective-permute-start(bf16[1024,256]{1,0:T(8,128)(2,1)} %get-tuple-element.55), channel_id=1, source_target_pairs={{0,3},{1,0},{2,1},{3,2},{4,7},{5,4},{6,5},{7,6},{8,11},{9,8},{10,9... | collective-permute-start | bytes 1572872 | tf_op jit(solution)/shard_map/ppermute | solution.py:40
  135.1 1.3 collective-permute-start.25
  136.3 4.8 %collective-permute-done.21.refs_0_.refs_7_ = bf16[1024,256]{1,0:T(8,128)(2,1)S(1)} collective-permute-done((bf16[1024,256]{1,0:T(8,128)(2,1)}, bf16[1024,256]{1,0:T(8,128)(2,1)S(1)}, u32[]{:S(2)}, u32[]{:S(2)}) %collective-permute-start.21) | collective-permute-done | bytes 524320 | tf_op jit(solution)/shard_map/ppermute | solution.py:40
  141.1 6.1 %collective-permute-done.28 = bf16[1024,256]{1,0:T(8,128)(2,1)S(1)} collective-permute-done((bf16[1024,256]{1,0:T(8,128)(2,1)}, bf16[1024,256]{1,0:T(8,128)(2,1)S(1)}, u32[]{:S(2)}, u32[]{:S(2)}) %collective-permute-start.28) | collective-permute-done | bytes 524320 | tf_op jit(solution)/shard_map/ppermute | solution.py:40
  147.2 3.6 %collective-permute-start.30 = (bf16[1024,256]{1,0:T(8,128)(2,1)S(1)}, bf16[1024,256]{1,0:T(8,128)(2,1)}, u32[]{:S(2)}, u32[]{:S(2)}) collective-permute-start(bf16[1024,256]{1,0:T(8,128)(2,1)S(1)} %collective-permute-done.28), channel_id=1, source_target_pairs={{0,3},{1,0},{2,1},{3,2},{4,7},{5,4},{6,5},{7,6},{8,11},{9,8},{10,9... | collective-permute-start | bytes 1572872 | tf_op jit(solution)/shard_map/ppermute | solution.py:40
  151.7 1.3 collective-permute-start.27
  153.0 9.2 %collective-permute-done.22.refs_1_ = bf16[1024,256]{1,0:T(8,128)(2,1)S(1)} collective-permute-done((bf16[1024,256]{1,0:T(8,128)(2,1)S(1)}, bf16[1024,256]{1,0:T(8,128)(2,1)S(1)}, u32[]{:S(2)}, u32[]{:S(2)}) %collective-permute-start.22) | collective-permute-done | bytes 524320 | tf_op jit(solution)/shard_map/ppermute | solution.py:40
  162.2 0.8 collective-permute-done.30
  164.3 9.3 %collective-permute-done.23.refs_2_ = bf16[1024,256]{1,0:T(8,128)(2,1)} collective-permute-done((bf16[1024,256]{1,0:T(8,128)(2,1)S(1)}, bf16[1024,256]{1,0:T(8,128)(2,1)}, u32[]{:S(2)}, u32[]{:S(2)}) %collective-permute-start.23) | collective-permute-done | bytes 524320 | tf_op jit(solution)/shard_map/ppermute | solution.py:40
  173.7 3.8 %collective-permute-done.24.refs_3_ = bf16[1024,256]{1,0:T(8,128)(2,1)} collective-permute-done((bf16[1024,256]{1,0:T(8,128)(2,1)S(1)}, bf16[1024,256]{1,0:T(8,128)(2,1)}, u32[]{:S(2)}, u32[]{:S(2)}) %collective-permute-start.24) | collective-permute-done | bytes 524320 | tf_op jit(solution)/shard_map/ppermute | solution.py:40
  177.5 28.0 %layer.3 = (bf16[1024,1024]{1,0:T(8,128)(2,1)}, bf16[4,128,256]{2,1,0:T(8,128)(2,1)}) custom-call(s32[3]{0:T(128)} %pad_add_fusion.1.where.refs_0_, f32[1,16]{1,0:T(1,128)} %bias_ref.3, bf16[1024,256]{1,0:T(8,128)(2,1)} %copy-done.5, bf16[1024,256]{1,0:T(8,128)(2,1)} %copy-done.21, bf16[1024,256]{1,0:T(8,128)(2,1)} %collective-permute-done.23.refs_2_, ...), custom_call_target="tpu_custom_call" | custom-call | flops 8589934592 | bytes 11018316 | tf_op jit(solution)/shard_map/layer/pallas_call | solution.py:66
  205.5 0.7 collective-permute-start.32
  206.2 2.4 collective-permute-start.33
  208.6 1.4 collective-permute-start.34
  210.1 5.0 %collective-permute-done.32.refs_2_ = bf16[4,128,256]{2,1,0:T(8,128)(2,1)S(1)} collective-permute-done((bf16[4,128,256]{2,1,0:T(8,128)(2,1)}, bf16[4,128,256]{2,1,0:T(8,128)(2,1)S(1)}, u32[]{:S(2)}, u32[]{:S(2)}) %collective-permute-start.32) | collective-permute-done | bytes 262176 | tf_op jit(solution)/shard_map/ppermute | solution.py:40
  215.0 2.2 collective-permute-done.33.refs_3_
  217.2 3.5 %collective-permute-done.34.refs_4_ = bf16[4,128,256]{2,1,0:T(8,128)(2,1)S(1)} collective-permute-done((bf16[4,128,256]{2,1,0:T(8,128)(2,1)}, bf16[4,128,256]{2,1,0:T(8,128)(2,1)S(1)}, u32[]{:S(2)}, u32[]{:S(2)}) %collective-permute-start.34) | collective-permute-done | bytes 262176 | tf_op jit(solution)/shard_map/ppermute | solution.py:40
  220.8 0.7 copy-done.12
  221.5 4.8 %finish_last.1 = (bf16[256,512]{1,0:T(8,128)(2,1)}, bf16[256,512]{1,0:T(8,128)(2,1)}, bf16[256,512]{1,0:T(8,128)(2,1)}, bf16[256,512]{1,0:T(8,128)(2,1)}) custom-call(s32[3]{0:T(128)} %pad_add_fusion.1.where.refs_0_, bf16[4,128,256]{2,1,0:T(8,128)(2,1)} %get-tuple-element.56.refs_1_, bf16[4,128,256]{2,1,0:T(8,128)(2,1)} %copy-done.10, ...), custom_call_target="tpu_custom_call" | custom-call | bytes 4456972 | tf_op jit(solution)/shard_map/finish_last/pallas_call | solution.py:66
  226.4 1.7 collective-permute-start.36
  228.1 1.5 collective-permute-start.37
  229.6 12.0 %collective-permute-done.35.refs_1_ = bf16[256,512]{1,0:T(8,128)(2,1)S(1)} collective-permute-done((bf16[256,512]{1,0:T(8,128)(2,1)}, bf16[256,512]{1,0:T(8,128)(2,1)S(1)}, u32[]{:S(2)}, u32[]{:S(2)}) %collective-permute-start.35) | collective-permute-done | bytes 262176 | tf_op jit(solution)/shard_map/ppermute | solution.py:40
  242.3 0.9 copy-done.4
  243.2 1.6 place.1
  (82 shorter events, 4.7 us)
Async XLA Ops:
  0.0 118.4 %copy-start = (f32[1,16,128,128]{3,2,1,0:T(8,128)S(1)}, f32[1,16,128,128]{3,2,1,0:T(8,128)}, u32[]{:S(2)}) copy-start(f32[1,16,128,128]{3,2,1,0:T(8,128)} %param.14) | copy-start | bytes 3145732
  1.0 1.4 copy-start.1
  3.3 38.2 %copy-start.20 = (bf16[1,256,2048]{2,1,0:T(8,128)(2,1)S(1)}, bf16[1,256,2048]{2,1,0:T(8,128)(2,1)}, u32[]{:S(2)}) copy-start(bf16[1,256,2048]{2,1,0:T(8,128)(2,1)} %param.8) | copy-start | bytes 3145732
  3.3 8.7 %collective-permute-start = (bf16[128,896]{1,0:T(8,128)(2,1)S(1)}, bf16[128,896]{1,0:T(8,128)(2,1)S(1)}, u32[]{:S(2)}, u32[]{:S(2)}) collective-permute-start(bf16[128,896]{1,0:T(8,128)(2,1)S(1)} %get-tuple-element.35), channel_id=1, source_target_pairs={{0,1},{1,2},{2,3},{3,0},{4,5},{5,6},{6,7},{7,4},{8,9},{9,10},{10,1... | collective-permute-start | bytes 688136 | tf_op jit(solution)/shard_map/ppermute | solution.py:40
  5.0 13.1 %collective-permute-start.1 = (bf16[128,896]{1,0:T(8,128)(2,1)S(1)}, bf16[128,896]{1,0:T(8,128)(2,1)S(1)}, u32[]{:S(2)}, u32[]{:S(2)}) collective-permute-start(bf16[128,896]{1,0:T(8,128)(2,1)S(1)} %get-tuple-element.36), channel_id=1, source_target_pairs={{0,2},{1,3},{2,0},{3,1},{4,6},{5,7},{6,4},{7,5},{8,10},{9,11},{10,... | collective-permute-start | bytes 688136 | tf_op jit(solution)/shard_map/ppermute | solution.py:40
  7.9 10.2 %collective-permute-start.2 = (bf16[128,896]{1,0:T(8,128)(2,1)S(1)}, bf16[128,896]{1,0:T(8,128)(2,1)S(1)}, u32[]{:S(2)}, u32[]{:S(2)}) collective-permute-start(bf16[128,896]{1,0:T(8,128)(2,1)S(1)} %get-tuple-element.37), channel_id=1, source_target_pairs={{0,3},{1,0},{2,1},{3,2},{4,7},{5,4},{6,5},{7,6},{8,11},{9,8},{10,9... | collective-permute-start | bytes 688136 | tf_op jit(solution)/shard_map/ppermute | solution.py:40
  18.2 48.4 %copy-start.2 = (bf16[512,896]{1,0:T(8,128)(2,1)}, bf16[512,896]{1,0:T(8,128)(2,1)S(1)}, u32[]{:S(2)}) copy-start(bf16[512,896]{1,0:T(8,128)(2,1)S(1)} %join.2.refs_6_.refs_9_) | copy-start | bytes 2752516
  18.2 23.4 %collective-permute-start.3 = (bf16[512,896]{1,0:T(8,128)(2,1)S(1)}, bf16[512,896]{1,0:T(8,128)(2,1)S(1)}, u32[]{:S(2)}, u32[]{:S(2)}) collective-permute-start(bf16[512,896]{1,0:T(8,128)(2,1)S(1)} %join.2.refs_6_.refs_9_), channel_id=1, source_target_pairs={{0,4},{4,8},{8,12},{12,0},{1,5},{5,9},{9,13},{13,1},{2,6},{6,10},{... | collective-permute-start | bytes 2752520 | tf_op jit(solution)/shard_map/ppermute | solution.py:40
  20.2 21.4 %collective-permute-start.4 = (bf16[512,896]{1,0:T(8,128)(2,1)S(1)}, bf16[512,896]{1,0:T(8,128)(2,1)S(1)}, u32[]{:S(2)}, u32[]{:S(2)}) collective-permute-start(bf16[512,896]{1,0:T(8,128)(2,1)S(1)} %join.2.refs_6_.refs_9_), channel_id=1, source_target_pairs={{0,12},{4,0},{8,4},{12,8},{1,13},{5,1},{9,5},{13,9},{2,14},{6,2},{... | collective-permute-start | bytes 2752520 | tf_op jit(solution)/shard_map/ppermute | solution.py:40
  20.3 7.1 %collective-permute-start.5 = (bf16[128,768]{1,0:T(8,128)(2,1)S(1)}, bf16[128,768]{1,0:T(8,128)(2,1)S(1)}, u32[]{:S(2)}, u32[]{:S(2)}) collective-permute-start(bf16[128,768]{1,0:T(8,128)(2,1)S(1)} %get-tuple-element.42), channel_id=1, source_target_pairs={{0,1},{1,2},{2,3},{3,0},{4,5},{5,6},{6,7},{7,4},{8,9},{9,10},{10,1... | collective-permute-start | bytes 589832 | tf_op jit(solution)/shard_map/ppermute | solution.py:40
  21.5 11.0 %collective-permute-start.6 = (bf16[128,768]{1,0:T(8,128)(2,1)S(1)}, bf16[128,768]{1,0:T(8,128)(2,1)S(1)}, u32[]{:S(2)}, u32[]{:S(2)}) collective-permute-start(bf16[128,768]{1,0:T(8,128)(2,1)S(1)} %get-tuple-element.43), channel_id=1, source_target_pairs={{0,2},{1,3},{2,0},{3,1},{4,6},{5,7},{6,4},{7,5},{8,10},{9,11},{10,... | collective-permute-start | bytes 589832 | tf_op jit(solution)/shard_map/ppermute | solution.py:40
  23.9 8.6 %collective-permute-start.7 = (bf16[128,768]{1,0:T(8,128)(2,1)S(1)}, bf16[128,768]{1,0:T(8,128)(2,1)S(1)}, u32[]{:S(2)}, u32[]{:S(2)}) collective-permute-start(bf16[128,768]{1,0:T(8,128)(2,1)S(1)} %get-tuple-element.44), channel_id=1, source_target_pairs={{0,3},{1,0},{2,1},{3,2},{4,7},{5,4},{6,5},{7,6},{8,11},{9,8},{10,9... | collective-permute-start | bytes 589832 | tf_op jit(solution)/shard_map/ppermute | solution.py:40
  32.6 39.7 %copy-start.3 = (bf16[512,768]{1,0:T(8,128)(2,1)}, bf16[512,768]{1,0:T(8,128)(2,1)S(1)}, u32[]{:S(2)}) copy-start(bf16[512,768]{1,0:T(8,128)(2,1)S(1)} %join.3.refs_11_.refs_14_) | copy-start | bytes 2359300
  32.6 25.8 %collective-permute-start.10 = (bf16[512,768]{1,0:T(8,128)(2,1)S(1)}, bf16[512,768]{1,0:T(8,128)(2,1)S(1)}, u32[]{:S(2)}, u32[]{:S(2)}) collective-permute-start(bf16[512,768]{1,0:T(8,128)(2,1)S(1)} %join.3.refs_11_.refs_14_), channel_id=1, source_target_pairs={{0,4},{4,8},{8,12},{12,0},{1,5},{5,9},{9,13},{13,1},{2,6},{6,10},{... | collective-permute-start | bytes 2359304 | tf_op jit(solution)/shard_map/ppermute | solution.py:40
  41.5 30.7 %copy-start.15 = (bf16[512,896]{1,0:T(8,128)(2,1)}, bf16[512,896]{1,0:T(8,128)(2,1)S(1)}, u32[]{:S(2)}) copy-start(bf16[512,896]{1,0:T(8,128)(2,1)S(1)} %collective-permute-done.3.refs_7_.refs_10_) | copy-start | bytes 2752516
  41.5 30.8 %copy-start.16 = (bf16[512,896]{1,0:T(8,128)(2,1)}, bf16[512,896]{1,0:T(8,128)(2,1)S(1)}, u32[]{:S(2)}) copy-start(bf16[512,896]{1,0:T(8,128)(2,1)S(1)} %collective-permute-done.4.refs_8_.refs_11_) | copy-start | bytes 2752516
  41.6 24.9 %collective-permute-start.8 = (bf16[256,2048]{1,0:T(8,128)(2,1)S(1)}, bf16[256,2048]{1,0:T(8,128)(2,1)S(1)}, u32[]{:S(2)}, u32[]{:S(2)}) collective-permute-start(bf16[256,2048]{1,0:T(8,128)(2,1)S(1)} %bitcast.15), channel_id=1, source_target_pairs={{0,1},{1,2},{2,3},{3,0},{4,5},{5,6},{6,7},{7,4},{8,9},{9,10},{10,1... | collective-permute-start | bytes 3145736 | tf_op jit(solution)/shard_map/ppermute | solution.py:40
  42.9 23.6 %collective-permute-start.9 = (bf16[256,2048]{1,0:T(8,128)(2,1)S(1)}, bf16[256,2048]{1,0:T(8,128)(2,1)S(1)}, u32[]{:S(2)}, u32[]{:S(2)}) collective-permute-start(bf16[256,2048]{1,0:T(8,128)(2,1)S(1)} %bitcast.16), channel_id=1, source_target_pairs={{0,3},{1,0},{2,1},{3,2},{4,7},{5,4},{6,5},{7,6},{8,11},{9,8},{10,9... | collective-permute-start | bytes 3145736 | tf_op jit(solution)/shard_map/ppermute | solution.py:40
  44.9 20.5 %collective-permute-start.11 = (bf16[512,768]{1,0:T(8,128)(2,1)S(1)}, bf16[512,768]{1,0:T(8,128)(2,1)S(1)}, u32[]{:S(2)}, u32[]{:S(2)}) collective-permute-start(bf16[512,768]{1,0:T(8,128)(2,1)S(1)} %join.3.refs_11_.refs_14_), channel_id=1, source_target_pairs={{0,12},{4,0},{8,4},{12,8},{1,13},{5,1},{9,5},{13,9},{2,14},{6,2},{... | collective-permute-start | bytes 2359304 | tf_op jit(solution)/shard_map/ppermute | solution.py:40
  47.0 27.7 %copy-start.19 = (s32[2,1]{0,1:T(1,128)S(1)}, s32[2,1]{0,1:T(1,128)}, u32[]{:S(2)}) copy-start(s32[2,1]{0,1:T(1,128)} %param.15) | copy-start | bytes 28
  47.0 22.9 %collective-permute-start.14 = (bf16[256,896]{1,0:T(8,128)(2,1)S(1)}, bf16[256,896]{1,0:T(8,128)(2,1)S(1)}, u32[]{:S(2)}, u32[]{:S(2)}) collective-permute-start(bf16[256,896]{1,0:T(8,128)(2,1)S(1)} %slice.32), channel_id=1, source_target_pairs={{0,4},{4,8},{8,12},{12,0},{1,5},{5,9},{9,13},{13,1},{2,6},{6,10},{... | collective-permute-start | bytes 1376264 | tf_op jit(solution)/shard_map/ppermute | solution.py:40
  58.4 15.8 %copy-start.17 = (bf16[512,768]{1,0:T(8,128)(2,1)}, bf16[512,768]{1,0:T(8,128)(2,1)S(1)}, u32[]{:S(2)}) copy-start(bf16[512,768]{1,0:T(8,128)(2,1)S(1)} %collective-permute-done.10.refs_12_.refs_15_) | copy-start | bytes 2359300
  58.4 13.8 %collective-permute-start.15 = (bf16[256,896]{1,0:T(8,128)(2,1)S(1)}, bf16[256,896]{1,0:T(8,128)(2,1)S(1)}, u32[]{:S(2)}, u32[]{:S(2)}) collective-permute-start(bf16[256,896]{1,0:T(8,128)(2,1)S(1)} %slice.33), channel_id=1, source_target_pairs={{0,12},{4,0},{8,4},{12,8},{1,13},{5,1},{9,5},{13,9},{2,14},{6,2},{... | collective-permute-start | bytes 1376264 | tf_op jit(solution)/shard_map/ppermute | solution.py:40
  65.3 8.9 %copy-start.18 = (bf16[512,768]{1,0:T(8,128)(2,1)}, bf16[512,768]{1,0:T(8,128)(2,1)S(1)}, u32[]{:S(2)}) copy-start(bf16[512,768]{1,0:T(8,128)(2,1)S(1)} %collective-permute-done.11.refs_13_.refs_16_) | copy-start | bytes 2359300
  66.5 7.7 %copy-start.13 = (bf16[256,2048]{1,0:T(8,128)(2,1)}, bf16[256,2048]{1,0:T(8,128)(2,1)S(1)}, u32[]{:S(2)}) copy-start(bf16[256,2048]{1,0:T(8,128)(2,1)S(1)} %collective-permute-done.8.refs_1_) | copy-start | bytes 3145732
  66.5 7.7 %copy-start.14 = (bf16[256,2048]{1,0:T(8,128)(2,1)}, bf16[256,2048]{1,0:T(8,128)(2,1)S(1)}, u32[]{:S(2)}) copy-start(bf16[256,2048]{1,0:T(8,128)(2,1)S(1)} %collective-permute-done.9.refs_2_) | copy-start | bytes 3145732
  66.6 17.0 %collective-permute-start.12 = (bf16[128,2048]{1,0:T(8,128)(2,1)S(1)}, bf16[128,2048]{1,0:T(8,128)(2,1)}, u32[]{:S(2)}, u32[]{:S(2)}) collective-permute-start(bf16[128,2048]{1,0:T(8,128)(2,1)S(1)} %slice.26), channel_id=1, source_target_pairs={{0,1},{1,2},{2,3},{3,0},{4,5},{5,6},{6,7},{7,4},{8,9},{9,10},{10,1... | collective-permute-start | bytes 1572872 | tf_op jit(solution)/shard_map/ppermute | solution.py:40
  67.8 15.8 %collective-permute-start.13 = (bf16[128,2048]{1,0:T(8,128)(2,1)S(1)}, bf16[128,2048]{1,0:T(8,128)(2,1)}, u32[]{:S(2)}, u32[]{:S(2)}) collective-permute-start(bf16[128,2048]{1,0:T(8,128)(2,1)S(1)} %slice.27), channel_id=1, source_target_pairs={{0,3},{1,0},{2,1},{3,2},{4,7},{5,4},{6,5},{7,6},{8,11},{9,8},{10,9... | collective-permute-start | bytes 1572872 | tf_op jit(solution)/shard_map/ppermute | solution.py:40
  70.0 4.2 %copy-start.22 = (bf16[256,896]{1,0:T(8,128)(2,1)}, bf16[256,896]{1,0:T(8,128)(2,1)S(1)}, u32[]{:S(2)}) copy-start(bf16[256,896]{1,0:T(8,128)(2,1)S(1)} %collective-permute-done.14.refs_9_.refs_12_) | copy-start | bytes 1376260
  72.2 2.0 copy-start.23
  72.3 8.4 %collective-permute-start.16 = (bf16[256,768]{1,0:T(8,128)(2,1)S(1)}, bf16[256,768]{1,0:T(8,128)(2,1)}, u32[]{:S(2)}, u32[]{:S(2)}) collective-permute-start(bf16[256,768]{1,0:T(8,128)(2,1)S(1)} %slice.30), channel_id=1, source_target_pairs={{0,4},{4,8},{8,12},{12,0},{1,5},{5,9},{9,13},{13,1},{2,6},{6,10},{... | collective-permute-start | bytes 1179656 | tf_op jit(solution)/shard_map/ppermute | solution.py:40
  74.2 9.4 %collective-permute-start.17 = (bf16[256,768]{1,0:T(8,128)(2,1)S(1)}, bf16[256,768]{1,0:T(8,128)(2,1)S(1)}, u32[]{:S(2)}, u32[]{:S(2)}) collective-permute-start(bf16[256,768]{1,0:T(8,128)(2,1)S(1)} %slice.31), channel_id=1, source_target_pairs={{0,12},{4,0},{8,4},{12,8},{1,13},{5,1},{9,5},{13,9},{2,14},{6,2},{... | collective-permute-start | bytes 1179656 | tf_op jit(solution)/shard_map/ppermute | solution.py:40
  83.6 0.8 copy-start.24
  112.7 8.0 %collective-permute-start.18 = (bf16[4,128,256]{2,1,0:T(8,128)(2,1)}, bf16[4,128,256]{2,1,0:T(8,128)(2,1)S(1)}, u32[]{:S(2)}, u32[]{:S(2)}) collective-permute-start(bf16[4,128,256]{2,1,0:T(8,128)(2,1)} %get-tuple-element.51.refs_1_), channel_id=1, source_target_pairs={{0,4},{4,8},{8,12},{12,0},{1,5},{5,9},{9,13},{13,1},{2,6},{6,10},{... | collective-permute-start | bytes 786440 | tf_op jit(solution)/shard_map/ppermute | solution.py:40
  114.5 8.7 %collective-permute-start.19 = (bf16[4,128,256]{2,1,0:T(8,128)(2,1)}, bf16[4,128,256]{2,1,0:T(8,128)(2,1)S(1)}, u32[]{:S(2)}, u32[]{:S(2)}) collective-permute-start(bf16[4,128,256]{2,1,0:T(8,128)(2,1)} %get-tuple-element.51.refs_1_), channel_id=1, source_target_pairs={{0,8},{4,12},{8,0},{12,4},{1,9},{5,13},{9,1},{13,5},{2,10},{6,14},... | collective-permute-start | bytes 786440 | tf_op jit(solution)/shard_map/ppermute | solution.py:40
  115.9 10.0 %collective-permute-start.20 = (bf16[4,128,256]{2,1,0:T(8,128)(2,1)}, bf16[4,128,256]{2,1,0:T(8,128)(2,1)S(1)}, u32[]{:S(2)}, u32[]{:S(2)}) collective-permute-start(bf16[4,128,256]{2,1,0:T(8,128)(2,1)} %get-tuple-element.51.refs_1_), channel_id=1, source_target_pairs={{0,12},{4,0},{8,4},{12,8},{1,13},{5,1},{9,5},{13,9},{2,14},{6,2},{... | collective-permute-start | bytes 786440 | tf_op jit(solution)/shard_map/ppermute | solution.py:40
  120.8 5.1 %copy-start.7 = (bf16[4,128,256]{2,1,0:T(8,128)(2,1)}, bf16[4,128,256]{2,1,0:T(8,128)(2,1)S(1)}, u32[]{:S(2)}) copy-start(bf16[4,128,256]{2,1,0:T(8,128)(2,1)S(1)} %collective-permute-done.18.refs_2_) | copy-start | bytes 786436
  123.2 2.7 %copy-start.8 = (bf16[4,128,256]{2,1,0:T(8,128)(2,1)}, bf16[4,128,256]{2,1,0:T(8,128)(2,1)S(1)}, u32[]{:S(2)}) copy-start(bf16[4,128,256]{2,1,0:T(8,128)(2,1)S(1)} %collective-permute-done.19.refs_3_) | copy-start | bytes 786436
  125.9 0.7 copy-start.9
  132.2 8.8 %collective-permute-start.21 = (bf16[1024,256]{1,0:T(8,128)(2,1)}, bf16[1024,256]{1,0:T(8,128)(2,1)S(1)}, u32[]{:S(2)}, u32[]{:S(2)}) collective-permute-start(bf16[1024,256]{1,0:T(8,128)(2,1)} %get-tuple-element.54), channel_id=1, source_target_pairs={{0,16},{16,32},{32,48},{48,64},{64,80},{80,96},{96,112},{112,0},{1... | collective-permute-start | bytes 1572872 | tf_op jit(solution)/shard_map/ppermute | solution.py:40
  132.3 14.9 %collective-permute-start.28 = (bf16[1024,256]{1,0:T(8,128)(2,1)}, bf16[1024,256]{1,0:T(8,128)(2,1)S(1)}, u32[]{:S(2)}, u32[]{:S(2)}) collective-permute-start(bf16[1024,256]{1,0:T(8,128)(2,1)} %get-tuple-element.55), channel_id=1, source_target_pairs={{0,3},{1,0},{2,1},{3,2},{4,7},{5,4},{6,5},{7,6},{8,11},{9,8},{10,9... | collective-permute-start | bytes 1572872 | tf_op jit(solution)/shard_map/ppermute | solution.py:40
  135.1 16.0 %collective-permute-start.26 = (bf16[1024,256]{1,0:T(8,128)(2,1)}, bf16[1024,256]{1,0:T(8,128)(2,1)}, u32[]{:S(2)}, u32[]{:S(2)}) collective-permute-start(bf16[1024,256]{1,0:T(8,128)(2,1)} %get-tuple-element.55), channel_id=1, source_target_pairs={{0,1},{1,2},{2,3},{3,0},{4,5},{5,6},{6,7},{7,4},{8,9},{9,10},{10,1... | collective-permute-start | bytes 1572872 | tf_op jit(solution)/shard_map/ppermute | solution.py:40
  135.1 16.6 %collective-permute-start.25 = (bf16[1024,256]{1,0:T(8,128)(2,1)}, bf16[1024,256]{1,0:T(8,128)(2,1)S(1)}, u32[]{:S(2)}, u32[]{:S(2)}) collective-permute-start(bf16[1024,256]{1,0:T(8,128)(2,1)} %get-tuple-element.55), channel_id=1, source_target_pairs={{0,16},{16,32},{32,48},{48,64},{64,80},{80,96},{96,112},{112,0},{1... | collective-permute-start | bytes 1572872 | tf_op jit(solution)/shard_map/ppermute | solution.py:40
  141.1 36.4 %copy-start.5 = (bf16[1024,256]{1,0:T(8,128)(2,1)}, bf16[1024,256]{1,0:T(8,128)(2,1)S(1)}, u32[]{:S(2)}) copy-start(bf16[1024,256]{1,0:T(8,128)(2,1)S(1)} %collective-permute-done.21.refs_0_.refs_7_) | copy-start | bytes 1572868
  141.1 21.2 %collective-permute-start.22 = (bf16[1024,256]{1,0:T(8,128)(2,1)S(1)}, bf16[1024,256]{1,0:T(8,128)(2,1)S(1)}, u32[]{:S(2)}, u32[]{:S(2)}) collective-permute-start(bf16[1024,256]{1,0:T(8,128)(2,1)S(1)} %collective-permute-done.21.refs_0_.refs_7_), channel_id=1, source_target_pairs={{0,1},{1,2},{2,3},{3,0},{4,5},{5,6},{6,7},{7,4},{8,9},{9,10},{10,1... | collective-permute-start | bytes 1572872 | tf_op jit(solution)/shard_map/ppermute | solution.py:40
  147.2 15.9 %collective-permute-start.30 = (bf16[1024,256]{1,0:T(8,128)(2,1)S(1)}, bf16[1024,256]{1,0:T(8,128)(2,1)}, u32[]{:S(2)}, u32[]{:S(2)}) collective-permute-start(bf16[1024,256]{1,0:T(8,128)(2,1)S(1)} %collective-permute-done.28), channel_id=1, source_target_pairs={{0,3},{1,0},{2,1},{3,2},{4,7},{5,4},{6,5},{7,6},{8,11},{9,8},{10,9... | collective-permute-start | bytes 1572872 | tf_op jit(solution)/shard_map/ppermute | solution.py:40
  150.8 22.9 %collective-permute-start.23 = (bf16[1024,256]{1,0:T(8,128)(2,1)S(1)}, bf16[1024,256]{1,0:T(8,128)(2,1)}, u32[]{:S(2)}, u32[]{:S(2)}) collective-permute-start(bf16[1024,256]{1,0:T(8,128)(2,1)S(1)} %collective-permute-done.21.refs_0_.refs_7_), channel_id=1, source_target_pairs={{0,3},{1,0},{2,1},{3,2},{4,7},{5,4},{6,5},{7,6},{8,11},{9,8},{10,9... | collective-permute-start | bytes 1572872 | tf_op jit(solution)/shard_map/ppermute | solution.py:40
  151.1 22.6 %collective-permute-start.29 = (bf16[1024,256]{1,0:T(8,128)(2,1)S(1)}, bf16[1024,256]{1,0:T(8,128)(2,1)}, u32[]{:S(2)}, u32[]{:S(2)}) collective-permute-start(bf16[1024,256]{1,0:T(8,128)(2,1)S(1)} %collective-permute-done.28), channel_id=1, source_target_pairs={{0,16},{16,32},{32,48},{48,64},{64,80},{80,96},{96,112},{112,0},{1... | collective-permute-start | bytes 1572872 | tf_op jit(solution)/shard_map/ppermute | solution.py:40
  151.7 25.8 %copy-start.6 = (bf16[1024,256]{1,0:T(8,128)(2,1)}, bf16[1024,256]{1,0:T(8,128)(2,1)S(1)}, u32[]{:S(2)}) copy-start(bf16[1024,256]{1,0:T(8,128)(2,1)S(1)} %collective-permute-done.25.refs_4_.refs_8_) | copy-start | bytes 1572868
  151.7 22.0 %collective-permute-start.27 = (bf16[1024,256]{1,0:T(8,128)(2,1)}, bf16[1024,256]{1,0:T(8,128)(2,1)}, u32[]{:S(2)}, u32[]{:S(2)}) collective-permute-start(bf16[1024,256]{1,0:T(8,128)(2,1)} %collective-permute-done.26), channel_id=1, source_target_pairs={{0,16},{16,32},{32,48},{48,64},{64,80},{80,96},{96,112},{112,0},{1... | collective-permute-start | bytes 1572872 | tf_op jit(solution)/shard_map/ppermute | solution.py:40
  162.2 15.3 %copy-start.21 = (bf16[1024,256]{1,0:T(8,128)(2,1)}, bf16[1024,256]{1,0:T(8,128)(2,1)S(1)}, u32[]{:S(2)}) copy-start(bf16[1024,256]{1,0:T(8,128)(2,1)S(1)} %collective-permute-done.22.refs_1_) | copy-start | bytes 1572868
  162.2 15.3 %collective-permute-start.24 = (bf16[1024,256]{1,0:T(8,128)(2,1)S(1)}, bf16[1024,256]{1,0:T(8,128)(2,1)}, u32[]{:S(2)}, u32[]{:S(2)}) collective-permute-start(bf16[1024,256]{1,0:T(8,128)(2,1)S(1)} %collective-permute-done.22.refs_1_), channel_id=1, source_target_pairs={{0,1},{1,2},{2,3},{3,0},{4,5},{5,6},{6,7},{7,4},{8,9},{9,10},{10,1... | collective-permute-start | bytes 1572872 | tf_op jit(solution)/shard_map/ppermute | solution.py:40
  163.0 14.4 %collective-permute-start.31 = (bf16[1024,256]{1,0:T(8,128)(2,1)}, bf16[1024,256]{1,0:T(8,128)(2,1)}, u32[]{:S(2)}, u32[]{:S(2)}) collective-permute-start(bf16[1024,256]{1,0:T(8,128)(2,1)} %collective-permute-done.30), channel_id=1, source_target_pairs={{0,16},{16,32},{32,48},{48,64},{64,80},{80,96},{96,112},{112,0},{1... | collective-permute-start | bytes 1572872 | tf_op jit(solution)/shard_map/ppermute | solution.py:40
  205.5 9.5 %collective-permute-start.32 = (bf16[4,128,256]{2,1,0:T(8,128)(2,1)}, bf16[4,128,256]{2,1,0:T(8,128)(2,1)S(1)}, u32[]{:S(2)}, u32[]{:S(2)}) collective-permute-start(bf16[4,128,256]{2,1,0:T(8,128)(2,1)} %get-tuple-element.56.refs_1_), channel_id=1, source_target_pairs={{0,4},{4,8},{8,12},{12,0},{1,5},{5,9},{9,13},{13,1},{2,6},{6,10},{... | collective-permute-start | bytes 786440 | tf_op jit(solution)/shard_map/ppermute | solution.py:40
  206.2 11.0 %collective-permute-start.33 = (bf16[4,128,256]{2,1,0:T(8,128)(2,1)}, bf16[4,128,256]{2,1,0:T(8,128)(2,1)S(1)}, u32[]{:S(2)}, u32[]{:S(2)}) collective-permute-start(bf16[4,128,256]{2,1,0:T(8,128)(2,1)} %get-tuple-element.56.refs_1_), channel_id=1, source_target_pairs={{0,8},{4,12},{8,0},{12,4},{1,9},{5,13},{9,1},{13,5},{2,10},{6,14},... | collective-permute-start | bytes 786440 | tf_op jit(solution)/shard_map/ppermute | solution.py:40
  208.6 12.2 %collective-permute-start.34 = (bf16[4,128,256]{2,1,0:T(8,128)(2,1)}, bf16[4,128,256]{2,1,0:T(8,128)(2,1)S(1)}, u32[]{:S(2)}, u32[]{:S(2)}) collective-permute-start(bf16[4,128,256]{2,1,0:T(8,128)(2,1)} %get-tuple-element.56.refs_1_), channel_id=1, source_target_pairs={{0,12},{4,0},{8,4},{12,8},{1,13},{5,1},{9,5},{13,9},{2,14},{6,2},{... | collective-permute-start | bytes 786440 | tf_op jit(solution)/shard_map/ppermute | solution.py:40
  215.0 5.8 %copy-start.10 = (bf16[4,128,256]{2,1,0:T(8,128)(2,1)}, bf16[4,128,256]{2,1,0:T(8,128)(2,1)S(1)}, u32[]{:S(2)}) copy-start(bf16[4,128,256]{2,1,0:T(8,128)(2,1)S(1)} %collective-permute-done.32.refs_2_) | copy-start | bytes 786436
  217.2 3.6 %copy-start.11 = (bf16[4,128,256]{2,1,0:T(8,128)(2,1)}, bf16[4,128,256]{2,1,0:T(8,128)(2,1)S(1)}, u32[]{:S(2)}) copy-start(bf16[4,128,256]{2,1,0:T(8,128)(2,1)S(1)} %collective-permute-done.33.refs_3_) | copy-start | bytes 786436
  220.8 0.7 copy-start.12
  226.3 15.3 %collective-permute-start.35 = (bf16[256,512]{1,0:T(8,128)(2,1)}, bf16[256,512]{1,0:T(8,128)(2,1)S(1)}, u32[]{:S(2)}, u32[]{:S(2)}) collective-permute-start(bf16[256,512]{1,0:T(8,128)(2,1)} %get-tuple-element.60), channel_id=1, source_target_pairs={{0,1},{1,2},{2,3},{3,0},{4,5},{5,6},{6,7},{7,4},{8,9},{9,10},{10,1... | collective-permute-start | bytes 786440 | tf_op jit(solution)/shard_map/ppermute | solution.py:40
  226.4 15.3 %collective-permute-start.36 = (bf16[256,512]{1,0:T(8,128)(2,1)}, bf16[256,512]{1,0:T(8,128)(2,1)S(1)}, u32[]{:S(2)}, u32[]{:S(2)}) collective-permute-start(bf16[256,512]{1,0:T(8,128)(2,1)} %get-tuple-element.61), channel_id=1, source_target_pairs={{0,2},{1,3},{2,0},{3,1},{4,6},{5,7},{6,4},{7,5},{8,10},{9,11},{10,... | collective-permute-start | bytes 786440 | tf_op jit(solution)/shard_map/ppermute | solution.py:40
  228.1 14.2 %collective-permute-start.37 = (bf16[256,512]{1,0:T(8,128)(2,1)}, bf16[256,512]{1,0:T(8,128)(2,1)S(1)}, u32[]{:S(2)}, u32[]{:S(2)}) collective-permute-start(bf16[256,512]{1,0:T(8,128)(2,1)} %get-tuple-element.62), channel_id=1, source_target_pairs={{0,3},{1,0},{2,1},{3,2},{4,7},{5,4},{6,5},{7,6},{8,11},{9,8},{10,9... | collective-permute-start | bytes 786440 | tf_op jit(solution)/shard_map/ppermute | solution.py:40
  242.3 1.0 copy-start.4
